TPU v7x, 128 devices: a whole 4x4x4 slice. The times are simulated.
128 devices in a mesh: agent: 2 (over x_hi), row: 8 (over x_lo, z), col: 8 (over y, core).
Axes of the slice: x: 4 (x_hi: 2, x_lo: 2; x = x_hi * 2 + x_lo), y: 4, z: 4, core: 2. Of those that a mesh axis runs over, the one named last changes fastest.
Arguments:
- probe_field: float32 [2, 256, 256], replicated, may hold values from -4.2 to 4.2
- offsets: int32 [2, 32, 16], P(None, ('agent', 'row'), 'col'), may hold values from -32 to 32
- amplitudes: float32 [32, 16, 256, 256], P(('agent', 'row'), 'col'), may hold values from 0.2 to 2
- data_state: float32 [2, 2048, 1024], P(None, ('agent', 'row'), 'col'), may hold values from -4.2 to 4.2
- prior_state: float32 [2, 2048, 1024], P(None, ('agent', 'row', 'col')), may hold values from -4.2 to 4.2
- first_weights: bfloat16 [3, 32, 6], replicated, may hold values from -2 to 2
- middle_weights: bfloat16 [4, 3, 32, 96], replicated, may hold values from -0.5 to 0.5
- last_weights: bfloat16 [3, 2, 96], replicated, may hold values from -0.375 to 0.375
Outputs:
- data_next: float32 [2, 2048, 1024], P(None, ('agent', 'row'), 'col')
- prior_next: float32 [2, 2048, 1024], P(None, ('agent', 'row', 'col'))
All inputs are finite; a program needn't handle non-finite values.
Results may differ from a plain program's by a relative error of at most 0.0073.
Values may be sent and summed in bfloat16 or wider, within the bound.
A program may use at most 64 MiB of HBM per device.

v0:
```python
import math

import jax
import jax.numpy as jnp
from jax import lax
from jax.sharding import Mesh
from jax.sharding import PartitionSpec as P

PROBE = 256
STEP = 64
JITTER = 32
LAYERS = 6
HALO = 128
AGENT_ROW_COL = ("agent", "row", "col_0", "col_1")
COL = ("col_0", "col_1")


MAGNITUDE_FLOOR = 0.5
DATA_STEP = 0.125
DATA_WEIGHT = 0.6
RELAXATION = 0.5


def extended_2(block, sides, width):
    for axis, dim in sides:
        count = lax.axis_size(axis)
        forward = [(i, i + 1) for i in range(count - 1)]
        backward = [(target, source) for source, target in forward]
        low = lax.ppermute(
            lax.slice_in_dim(block, block.shape[dim] - width, None, axis=dim), axis, forward
        )
        high = lax.ppermute(lax.slice_in_dim(block, 0, width, axis=dim), axis, backward)
        block = jnp.concatenate([low, block, high], axis=dim)
    return block


def padded(value, sides, width):
    edges = {}
    for axis, dim in sides:
        size, length = (lax.axis_size(axis), value.shape[dim])
        up = [(i, (i + 1) % size) for i in range(size - 1)]
        last = lax.slice_in_dim(value, length - width, length, axis=dim)
        initial = lax.slice_in_dim(value, 0, width, axis=dim)
        edges[dim] = (
            lax.ppermute(last, axis, up),
            lax.ppermute(initial, axis, [(b, a) for a, b in up]),
        )
    done = []
    for _, dim in sides:
        low, high = edges[dim]
        around = [(width, width) if d in done else (0, 0) for d in range(value.ndim)]
        value = jnp.concatenate([jnp.pad(low, around), value, jnp.pad(high, around)], axis=dim)
        done.append(dim)
    return value


def cut_along(value, dim, size):
    before, after = (value.shape[:dim], value.shape[dim + 1 :])
    return jnp.moveaxis(value.reshape(*before, size, -1, *after), dim, 0)


def in_order(blocks, dim):
    lengths = list(blocks.shape[1:])
    lengths[dim] *= blocks.shape[0]
    return jnp.moveaxis(blocks, 0, dim).reshape(lengths)


def moved_by_axis(blocks, axes, order):
    inside = blocks.shape[1:]
    whole = blocks.reshape(*(lax.axis_size(a) for a in axes), *inside)
    for k in order:
        whole = lax.all_to_all(whole, axes[k], k, k, tiled=True)
    return whole.reshape(-1, *inside)


def one_axis_at_a_time(value, axes, order, split_dim, concat_dim):
    blocks = cut_along(value, split_dim, lax.axis_size(axes))
    return in_order(moved_by_axis(blocks, axes, order), concat_dim)


def as_index(value):
    return jnp.asarray(value).astype(jnp.int32)


def dft_tables():
    numbers = jnp.arange(PROBE, dtype=jnp.int32)
    product = numbers[:, None] * numbers[None, :] % PROBE
    angles = product.astype(jnp.float32) * (2.0 * math.pi / PROBE)
    scaling = 1.0 / math.sqrt(PROBE)
    return (
        (jnp.cos(angles) * scaling).astype(jnp.bfloat16),
        (-jnp.sin(angles) * scaling).astype(jnp.bfloat16),
    )


def right_product(left_real, left_imag, table_real, table_imag):
    joined = jnp.concatenate([left_real, left_imag], axis=-1)
    table = jnp.concatenate(
        [
            jnp.concatenate([table_real, table_imag], axis=1),
            jnp.concatenate([-table_imag, table_real], axis=1),
        ],
        axis=0,
    )
    output = jnp.einsum("bjk,kw->bjw", joined, table, preferred_element_type=jnp.float32)
    midpoint = left_real.shape[-1]
    return (output[..., :midpoint], output[..., midpoint:])


def left_product(table_real, table_imag, right_real, right_imag):
    stacked = jnp.concatenate([table_real, table_imag], axis=0)
    first = jnp.einsum("jk,bkw->bjw", stacked, right_real, preferred_element_type=jnp.float32)
    second = jnp.einsum("jk,bkw->bjw", stacked, right_imag, preferred_element_type=jnp.float32)
    midpoint = table_real.shape[0]
    return (first[:, :midpoint] - second[:, midpoint:], first[:, midpoint:] + second[:, :midpoint])


def position_terms(patches, measured, probe_field, table_real, table_imag):
    probe_real = probe_field[0]
    probe_imag = probe_field[1]
    object_real = patches[:, 0]
    object_imag = patches[:, 1]
    exit_real = (probe_real * object_real - probe_imag * object_imag).astype(jnp.bfloat16)
    exit_imag = (probe_real * object_imag + probe_imag * object_real).astype(jnp.bfloat16)
    half_real, half_imag = right_product(exit_real, exit_imag, table_real, table_imag)
    wave_real, wave_imag = left_product(
        table_real, table_imag, half_real.astype(jnp.bfloat16), half_imag.astype(jnp.bfloat16)
    )
    magnitude = jnp.sqrt(wave_real * wave_real + wave_imag * wave_imag)
    retained = 1.0 - measured / jnp.maximum(magnitude, MAGNITUDE_FLOOR)
    resid_real = (wave_real * retained).astype(jnp.bfloat16)
    resid_imag = (wave_imag * retained).astype(jnp.bfloat16)
    back_real, back_imag = right_product(resid_real, resid_imag, table_real, -table_imag)
    field_real, field_imag = left_product(
        table_real, -table_imag, back_real.astype(jnp.bfloat16), back_imag.astype(jnp.bfloat16)
    )
    contrib_real = probe_real * field_real + probe_imag * field_imag
    contrib_imag = probe_real * field_imag - probe_imag * field_real
    return jnp.stack([contrib_real, contrib_imag], axis=1)


def fold_margins(array, axis_dim, extent):
    centre = lax.slice_in_dim(array, 2 * HALO, 2 * HALO + extent, axis=axis_dim)
    lower = lax.slice_in_dim(array, 0, HALO, axis=axis_dim)
    upper = lax.slice_in_dim(array, extent + 3 * HALO, extent + 4 * HALO, axis=axis_dim)
    lower_pad = [(0, 0)] * array.ndim
    lower_pad[axis_dim] = (0, extent - HALO)
    upper_pad = [(0, 0)] * array.ndim
    upper_pad[axis_dim] = (extent - HALO, 0)
    return centre + lower + upper


def convolve(current, weight):
    row_count = current.shape[1] - 2
    col_count = current.shape[2]
    widened = jnp.pad(current, ((0, 0), (0, 0), (1, 1)))
    summed = None
    for shift_row in range(3):
        stacked = jnp.concatenate(
            [
                widened[:, shift_row : shift_row + row_count, shift_col : shift_col + col_count]
                for shift_col in range(3)
            ],
            axis=0,
        )
        contribution = jnp.einsum(
            "ok,krw->orw", weight[shift_row], stacked, preferred_element_type=jnp.float32
        )
        summed = contribution if summed is None else summed + contribution
    return summed


def denoise_rows(current, first_row, height, weights):
    output = None
    for depth in range(LAYERS):
        output = convolve(current, weights[depth])
        first_row = first_row + 1
        if depth < LAYERS - 1:
            row_ids = first_row + jnp.arange(output.shape[1], dtype=jnp.int32)
            inside = (row_ids >= 0) & (row_ids < height)
            current = jnp.where(inside[None, :, None], jax.nn.relu(output), 0.0).astype(
                jnp.bfloat16
            )
    return output


def on_device(
    probe_field,
    offsets,
    amplitudes,
    data_state,
    prior_state,
    first_weights,
    middle_weights,
    last_weights,
):
    table_real, table_imag = dft_tables()
    tile_rows = data_state.shape[1]
    tile_cols = data_state.shape[2]
    grid_rows = tile_rows // STEP
    grid_cols = tile_cols // STEP
    anchor_zero = as_index(0)
    extended = extended_2(data_state, ((("agent", "row"), 1), (COL, 2)), HALO)
    ext_rows = extended.shape[1]
    ext_cols = extended.shape[2]
    upper_grid = as_index(
        (jnp.arange(grid_rows, dtype=jnp.int32) * STEP + JITTER)[:, None] + offsets[0]
    )
    left_grid = as_index(
        (jnp.arange(grid_cols, dtype=jnp.int32) * STEP + JITTER)[None, :] + offsets[1]
    )
    upper_edges = upper_grid.reshape(-1)
    left_edges = left_grid.reshape(-1)
    patches = jax.vmap(
        lambda upper_edge, left_edge: lax.dynamic_slice(
            extended, (anchor_zero, as_index(upper_edge), as_index(left_edge)), (2, PROBE, PROBE)
        )
    )(upper_edges, left_edges)
    contributions = position_terms(
        patches, amplitudes.reshape(-1, PROBE, PROBE), probe_field, table_real, table_imag
    )
    contributions = contributions.reshape(grid_rows, grid_cols, 2, PROBE, PROBE)
    probe_ids = jnp.arange(PROBE, dtype=jnp.int32)
    row_ids = jnp.arange(ext_rows, dtype=jnp.int32)
    col_ids = jnp.arange(ext_cols, dtype=jnp.int32)

    def place_row(total, inputs):
        uppers, lefts, terms = inputs
        row_hit = (
            row_ids[None, :, None] == uppers[:, None, None] + probe_ids[None, None, :]
        ).astype(jnp.float32)
        col_hit = (
            lefts[:, None, None] + probe_ids[None, :, None] == col_ids[None, None, :]
        ).astype(jnp.float32)
        spread = jnp.einsum("gkab,gbc->gkac", terms, col_hit)
        placed = jnp.einsum("gra,gkac->krc", row_hit, spread)
        return (total + placed, None)

    buffer = lax.scan(
        place_row, jnp.zeros(extended.shape, jnp.float32), (upper_grid, left_grid, contributions)
    )[0]
    column_wide = extended_2(buffer, ((COL, 2),), HALO)
    folded = fold_margins(column_wide, 2, tile_cols)
    row_wide = padded(folded, ((("agent", "row"), 1),), HALO)
    gradient = fold_margins(row_wide, 1, tile_rows)
    data_update = data_state - DATA_STEP * gradient
    data_reflect = 2.0 * data_update - data_state
    weights = (
        [first_weights] + [middle_weights[number] for number in range(LAYERS - 2)] + [last_weights]
    )
    inputs = prior_state.astype(jnp.bfloat16)
    strip_rows = prior_state.shape[1]
    widened = extended_2(inputs, ((AGENT_ROW_COL, 1),), LAYERS)
    height = strip_rows * lax.axis_size(AGENT_ROW_COL)
    first_row = as_index(lax.axis_index(AGENT_ROW_COL) * strip_rows - LAYERS)
    noise = denoise_rows(widened, first_row, height, weights)
    prior_update = prior_state - noise
    prior_reflect = 2.0 * prior_update - prior_state
    reflect_tiles = one_axis_at_a_time(prior_reflect, COL, (1, 0), 2, 1)
    consensus = DATA_WEIGHT * data_reflect + (1.0 - DATA_WEIGHT) * reflect_tiles
    data_next = (1.0 - RELAXATION) * data_state + RELAXATION * (2.0 * consensus - data_reflect)
    consensus_strips = lax.all_to_all(consensus, COL, split_axis=1, concat_axis=2, tiled=True)
    prior_next = (1.0 - RELAXATION) * prior_state + RELAXATION * (
        2.0 * consensus_strips - prior_reflect
    )
    return (data_next, prior_next)


def solution(mesh):
    torus = Mesh(
        mesh.devices.reshape(mesh.shape["agent"], mesh.shape["row"], 4, 2),
        ("agent", "row", "col_0", "col_1"),
    )
    in_specs = (
        P(),
        P(None, ("agent", "row"), COL),
        P(("agent", "row"), COL, None, None),
        P(None, ("agent", "row"), COL),
        P(None, AGENT_ROW_COL, None),
        P(),
        P(),
        P(),
    )
    out_specs = (P(None, ("agent", "row"), COL), P(None, AGENT_ROW_COL, None))
    return jax.shard_map(
        on_device, mesh=torus, in_specs=in_specs, out_specs=out_specs, check_vma=False
    )
```

profile of v0, /device:TPU:6, one launch (start us, length us, event | category | flops | bytes accessed | tf_op | source)
XLA Modules:
  0.0 137.7 jit_solution(7856105256474964101)
XLA Ops:
  0.6 4.0 %collective-permute-start = (f32[2,128,128]{2,1,0:T(8,128)}, f32[2,128,128]{2,1,0:T(8,128)S(1)}, u32[]{:S(2)}, u32[]{:S(2)}) collective-permute-start(f32[2,128,128]{2,1,0:T(8,128)} %param.13), channel_id=1, source_target_pairs={{0,8},{8,16},{16,24},{24,32},{32,40},{40,48},{48,56},{56,64},{64,7... | collective-permute-start | bytes 393224 | tf_op jit(solution)/shard_map/ppermute | solution.py:29
  4.6 4.3 %collective-permute-start.1 = (f32[2,128,128]{2,1,0:T(8,128)}, f32[2,128,128]{2,1,0:T(8,128)S(1)}, u32[]{:S(2)}, u32[]{:S(2)}) collective-permute-start(f32[2,128,128]{2,1,0:T(8,128)} %param.13), channel_id=1, source_target_pairs={{8,0},{16,8},{24,16},{32,24},{40,32},{48,40},{56,48},{64,56},{72,6... | collective-permute-start | bytes 393224 | tf_op jit(solution)/shard_map/ppermute | solution.py:32
  8.9 1.0 copy.138
  10.0 5.3 %collective-permute-start.9 = (bf16[2,6,1024]{2,0,1:T(2,128)(2,1)S(1)}, bf16[2,6,1024]{2,0,1:T(2,128)(2,1)S(1)}, u32[]{:S(2)}, u32[]{:S(2)}) collective-permute-start(bf16[2,6,1024]{2,0,1:T(2,128)(2,1)S(1)} %get-tuple-element.232), channel_id=1, source_target_pairs={{1,0},{2,1},{3,2},{4,3},{5,4},{6,5},{7,6},{8,7},{9,8},{10,9},{11,1... | collective-permute-start | bytes 73736 | tf_op jit(solution)/shard_map/ppermute | solution.py:32
  15.2 1.9 %collective-permute-start.8 = (bf16[2,6,1024]{2,0,1:T(2,128)(2,1)S(1)}, bf16[2,6,1024]{2,0,1:T(2,128)(2,1)S(1)}, u32[]{:S(2)}, u32[]{:S(2)}) collective-permute-start(bf16[2,6,1024]{2,0,1:T(2,128)(2,1)S(1)} %get-tuple-element.231), channel_id=1, source_target_pairs={{0,1},{1,2},{2,3},{3,4},{4,5},{5,6},{6,7},{7,8},{8,9},{9,10},{10,1... | collective-permute-start | bytes 73736 | tf_op jit(solution)/shard_map/ppermute | solution.py:29
  17.2 1.1 multiply_convert_fusion.2
  18.3 1.0 fusion.218
  19.4 1.1 slice_bitcast_fusion.1
  21.2 0.8 bitcast_add_fusion.1
  22.8 1.8 %collective-permute-done.8 = bf16[2,6,1024]{2,0,1:T(2,128)(2,1)S(1)} collective-permute-done((bf16[2,6,1024]{2,0,1:T(2,128)(2,1)S(1)}, bf16[2,6,1024]{2,0,1:T(2,128)(2,1)S(1)}, u32[]{:S(2)}, u32[]{:S(2)}) %collective-permute-start.8) | collective-permute-done | bytes 24608 | tf_op jit(solution)/shard_map/ppermute | solution.py:29
  24.8 0.9 pad_slice_fusion.31
  27.1 1.5 %fusion.127 = bf16[32,26,1024]{2,0,1:T(8,128)(2,1)S(1)} fusion(f32[26,1024,32]{1,2,0:T(8,128)S(1)} %fusion.183, f32[26,1024,32]{1,2,0:T(8,128)S(1)} %fusion.189, pred[26]{0:T(512)(128)(4,1)S(1)} %compare_and_fusion, bf16[2,26,1024]{2,0,1:T(2,128)(2,1)S(1)} %get-tuple-element.226, bf16[2,26,1024]{2,0,1:T(2,128)(2,1)S(1)} %get-tuple-element.227, ...), kind=kOutput, calls=%fused_computation.123 | convolution fusion | flops 15441920 | bytes 8841728 | tf_op jit(solution)/shard_map/ok,krw->orw/dot_general | solution.py:166
  28.6 5.8 %pad_slice_fusion.3 = (bf16[32,24,1024]{2,0,1:T(8,128)(2,1)S(1)}, bf16[32,24,1024]{2,0,1:T(8,128)(2,1)S(1)}, bf16[32,24,1024]{2,0,1:T(8,128)(2,1)S(1)}, bf16[32,...) fusion(bf16[32,26,1024]{2,0,1:T(8,128)(2,1)S(1)} %fusion.127), kind=kLoop, calls=%fused_computation.133 | loop fusion | bytes 20578304 | tf_op jit(solution)/shard_map/slice | solution.py:161
  35.1 0.8 fusion.35
  35.9 1.3 fusion.128
  37.2 5.7 %pad_slice_fusion.9 = (bf16[32,22,1024]{2,0,1:T(8,128)(2,1)S(1)}, bf16[32,22,1024]{2,0,1:T(8,128)(2,1)S(1)}, bf16[32,22,1024]{2,0,1:T(8,128)(2,1)S(1)}, bf16[32,...) fusion(bf16[32,24,1024]{2,0,1:T(8,128)(2,1)S(1)} %fusion.128), kind=kLoop, calls=%fused_computation.139 | loop fusion | bytes 18874368 | tf_op jit(solution)/shard_map/slice | solution.py:161
  44.3 1.3 fusion.131
  45.6 4.9 %pad_slice_fusion.15 = (bf16[32,20,1024]{2,0,1:T(8,128)(2,1)S(1)}, bf16[32,20,1024]{2,0,1:T(8,128)(2,1)S(1)}, bf16[32,20,1024]{2,0,1:T(8,128)(2,1)S(1)}, bf16[32...) fusion(bf16[32,22,1024]{2,0,1:T(8,128)(2,1)S(1)} %fusion.131), kind=kLoop, calls=%fused_computation.152 | loop fusion | bytes 17170432 | tf_op jit(solution)/shard_map/slice | solution.py:161
  51.7 1.2 fusion.134
  53.0 4.3 %pad_slice_fusion.21 = (bf16[32,18,1024]{2,0,1:T(8,128)(2,1)S(1)}, bf16[32,18,1024]{2,0,1:T(8,128)(2,1)S(1)}, bf16[32,18,1024]{2,0,1:T(8,128)(2,1)S(1)}, bf16[32...) fusion(bf16[32,20,1024]{2,0,1:T(8,128)(2,1)S(1)} %fusion.134), kind=kLoop, calls=%fused_computation.182 | loop fusion | bytes 15466496 | tf_op jit(solution)/shard_map/slice | solution.py:161
  58.5 1.1 fusion.137
  59.7 1.3 collective-permute-start.3
  61.0 3.1 %collective-permute-start.2 = (f32[2,384,128]{2,1,0:T(8,128)S(1)}, f32[2,384,128]{2,1,0:T(8,128)S(1)}, u32[]{:S(2)}, u32[]{:S(2)}) collective-permute-start(f32[2,384,128]{2,1,0:T(8,128)S(1)} %constant_dynamic-update-slice_fusion), channel_id=1, source_target_pairs={{0,1},{1,2},{2,3},{3,4},{4,5},{5,6},{6,7},{8,9},{9,10},{10,11},{11... | collective-permute-start | bytes 1179656 | tf_op jit(solution)/shard_map/ppermute | solution.py:29
  64.1 6.1 %pad_slice_fusion.25 = (bf16[32,16,1024]{2,0,1:T(8,128)(2,1)}, bf16[32,16,1024]{2,0,1:T(8,128)(2,1)S(1)}, bf16[32,16,1024]{2,0,1:T(8,128)(2,1)}, bf16[32,16,1024...) fusion(bf16[32,18,1024]{2,0,1:T(8,128)(2,1)S(1)} %fusion.137), kind=kLoop, calls=%fused_computation.186 | loop fusion | bytes 13762560 | tf_op jit(solution)/shard_map/slice | solution.py:161
  70.1 1.4 %fusion.101 = f32[16,1024,2]{1,2,0:T(2,128)} fusion(bf16[32,16,1024]{2,0,1:T(8,128)(2,1)S(1)} %get-tuple-element.208, bf16[32,16,1024]{2,0,1:T(8,128)(2,1)S(1)} %get-tuple-element.214, bf16[32,16,1024]{2,0,1:T(8,128)(2,1)S(1)} %get-tuple-element.215, bf16[3,2,96]{2,1,0:T(2,128)(2,1)S(1)} %copy-done.10), kind=kOutput, calls=%fused_computation.96 | convolution fusion | flops 15728640 | bytes 3277312 | tf_op jit(solution)/shard_map/ok,krw->orw/dot_general | solution.py:166
  71.7 11.3 %while.14 = (s32[]{:T(128)}, f32[2,384,384]{2,1,0:T(8,128)S(1)}, s32[4,3]{1,0:T(4,128)S(1)}, f32[4,2,256,256]{3,2,0,1:T(8,128)}, s32[]{:T(128)}) while((s32[]{:T(128)}, f32[2,384,384]{2,1,0:T(8,128)S(1)}, s32[4,3]{1,0:T(4,128)S(1)}, f32[4,2,256,256]{3,2,0,1:T(8,128)}, s32[]{:T(128)}) %tuple.117), condition=%wide.while_cond, body=%wide.while_body.sunk | while | flops 2 | bytes 1049717 | solution.py:215
  72.3 2.2 %bitcast_dynamic-update-slice_fusion.2 = f32[4,2,256,256]{3,2,0,1:T(8,128)} fusion(f32[4,2,256,256]{3,2,0,1:T(8,128)} %get-tuple-element.313, s32[]{:T(128)S(6)} %copy.145, f32[2,384,384]{2,1,0:T(8,128)S(1)} %get-tuple-element.316, s32[]{:T(128)} %bitcast.221, s32[]{:T(128)} %bitcast.222), kind=kLoop, calls=%fused_computation.2.clone.1 | loop fusion | bytes 1049604 | tf_op jit(solution)/shard_map/vmap()/gather
  75.1 2.2 %bitcast_dynamic-update-slice_fusion.2 = f32[4,2,256,256]{3,2,0,1:T(8,128)} fusion(f32[4,2,256,256]{3,2,0,1:T(8,128)} %get-tuple-element.313, s32[]{:T(128)S(6)} %copy.145, f32[2,384,384]{2,1,0:T(8,128)S(1)} %get-tuple-element.316, s32[]{:T(128)} %bitcast.221, s32[]{:T(128)} %bitcast.222), kind=kLoop, calls=%fused_computation.2.clone.1 | loop fusion | bytes 1049604 | tf_op jit(solution)/shard_map/vmap()/gather
  78.0 2.2 %bitcast_dynamic-update-slice_fusion.2 = f32[4,2,256,256]{3,2,0,1:T(8,128)} fusion(f32[4,2,256,256]{3,2,0,1:T(8,128)} %get-tuple-element.313, s32[]{:T(128)S(6)} %copy.145, f32[2,384,384]{2,1,0:T(8,128)S(1)} %get-tuple-element.316, s32[]{:T(128)} %bitcast.221, s32[]{:T(128)} %bitcast.222), kind=kLoop, calls=%fused_computation.2.clone.1 | loop fusion | bytes 1049604 | tf_op jit(solution)/shard_map/vmap()/gather
  80.8 2.2 %bitcast_dynamic-update-slice_fusion.2 = f32[4,2,256,256]{3,2,0,1:T(8,128)} fusion(f32[4,2,256,256]{3,2,0,1:T(8,128)} %get-tuple-element.313, s32[]{:T(128)S(6)} %copy.145, f32[2,384,384]{2,1,0:T(8,128)S(1)} %get-tuple-element.316, s32[]{:T(128)} %bitcast.221, s32[]{:T(128)} %bitcast.222), kind=kLoop, calls=%fused_computation.2.clone.1 | loop fusion | bytes 1049604 | tf_op jit(solution)/shard_map/vmap()/gather
  83.0 1.8 %fusion.166 = (bf16[4,256,256]{2,1,0:T(8,128)(2,1)S(1)}, bf16[4,256,256]{2,1,0:T(8,128)(2,1)S(1)}) fusion(f32[4,2,256,256]{3,2,0,1:T(8,128)} %get-tuple-element.73, f32[256,256]{1,0:T(8,128)S(1)} %get-tuple-element.219, f32[256,256]{1,0:T(8,128)S(1)} %get-tuple-element.218), kind=kLoop, calls=%fused_computation.170 | loop fusion | flops 2097152 | bytes 3670016 | tf_op jit(solution)/shard_map/convert_element_type | solution.py:123
  89.4 1.2 copy-done
  90.5 2.7 %while.15 = (s32[]{:T(128)}, f32[2,384,384]{1,2,0:T(8,128)S(1)}, bf16[2,2,2,256,256]{4,3,1,2,0:T(8,128)(2,1)S(1)}, s32[2,2]{1,0:T(2,128)S(1)}, s32[2,2]{1,0:T(2,128)S(1)}, /*index=5*/s32[]{:T(128)}, s32[]{:T(128)}) while((s32[]{:T(128)}, f32[2,384,384]{1,2,0:T(8,128)S(1)}, bf16[2,2,2,256,256]{4,3,1,2,0:T(8,128)(2,1)S(1)}, ...), condition=%wide.region_1.2_spmd.clone.clone, body=%wide.region_0.1_spmd.clone.clone.sunk | while | flops 504300544 | bytes 2891927 | solution.py:239
  90.7 1.2 fusion.297
  92.0 1.2 fusion.297
  93.6 0.8 fusion.280
  94.4 1.3 collective-permute-start.5
  95.7 3.8 %collective-permute-start.4 = (f32[2,384,128]{2,1,0:T(8,128)S(1)}, f32[2,384,128]{2,1,0:T(8,128)}, u32[]{:S(2)}, u32[]{:S(2)}) collective-permute-start(f32[2,384,128]{2,1,0:T(8,128)S(1)} %get-tuple-element.205), channel_id=1, source_target_pairs={{0,1},{1,2},{2,3},{3,4},{4,5},{5,6},{6,7},{8,9},{9,10},{10,11},{11... | collective-permute-start | bytes 1179656 | tf_op jit(solution)/shard_map/ppermute | solution.py:29
  99.5 2.5 %fusion.155 = f32[16,1024,2]{1,2,0:T(2,128)S(1)} fusion(f32[16,1024,2]{1,2,0:T(2,128)} %fusion.101, bf16[32,16,1024]{2,0,1:T(8,128)(2,1)} %get-tuple-element.210, bf16[32,16,1024]{2,0,1:T(8,128)(2,1)} %get-tuple-element.213, bf16[32,16,1024]{2,0,1:T(8,128)(2,1)S(1)} %copy-done.5, bf16[3,2,96]{2,1,0:T(2,128)(2,1)S(1)} %copy-done.10), kind=kOutput, calls=%fused_computation.148 | convolution fusion | flops 15761408 | bytes 3408384 | tf_op jit(solution)/shard_map/ok,krw->orw/dot_general | solution.py:166
  102.0 0.8 fusion.152
  103.1 3.9 %all_to_all.19 = f32[4,2,2,16,128]{4,0,2,3,1:T(4,128)S(1)} all-to-all(f32[4,2,2,16,128]{4,0,2,3,1:T(4,128)S(1)} %copy.112), channel_id=1, replica_groups=mesh['agent'=2,'row'=8,'col_0'=4,'col_1'=2] {'col_1'}, dimensions={1} | all-to-all | bytes 262144 | tf_op jit(solution)/shard_map/all_to_all | solution.py:72
  107.7 3.3 %all-to-all-start.1 = ((f32[4,2,2,16,128]{4,1,2,3,0:T(2,128)}), f32[4,2,2,16,128]{4,1,2,3,0:T(2,128)S(1)}, u32[]{:S(2)}, u32[]{:S(2)}) async-start(f32[4,2,2,16,128]{4,1,2,3,0:T(2,128)} %copy.113), calls=%async_computation.1 | async-start | bytes 262144 | tf_op jit(solution)/shard_map/all_to_all | solution.py:72
  111.1 1.2 fusion.200
  112.3 3.9 %collective-permute-start.7 = (f32[2,128,128]{2,1,0:T(8,128)S(1)}, f32[2,128,128]{2,1,0:T(8,128)S(1)}, u32[]{:S(2)}, u32[]{:S(2)}) collective-permute-start(f32[2,128,128]{2,1,0:T(8,128)S(1)} %get-tuple-element.221), channel_id=1, source_target_pairs={{8,0},{16,8},{24,16},{32,24},{40,32},{48,40},{56,48},{64,56},{72,6... | collective-permute-start | bytes 393224 | tf_op jit(solution)/shard_map/ppermute | solution.py:46
  116.2 1.9 %collective-permute-start.6 = (f32[2,128,128]{2,1,0:T(8,128)S(1)}, f32[2,128,128]{2,1,0:T(8,128)S(1)}, u32[]{:S(2)}, u32[]{:S(2)}) collective-permute-start(f32[2,128,128]{2,1,0:T(8,128)S(1)} %get-tuple-element.220), channel_id=1, source_target_pairs={{0,8},{8,16},{16,24},{24,32},{32,40},{40,48},{48,56},{56,64},{64,7... | collective-permute-start | bytes 393224 | tf_op jit(solution)/shard_map/ppermute | solution.py:45
  118.2 1.5 %collective-permute-done.7 = f32[2,128,128]{2,1,0:T(8,128)S(1)} collective-permute-done((f32[2,128,128]{2,1,0:T(8,128)S(1)}, f32[2,128,128]{2,1,0:T(8,128)S(1)}, u32[]{:S(2)}, u32[]{:S(2)}) %collective-permute-start.7) | collective-permute-done | bytes 131104 | tf_op jit(solution)/shard_map/ppermute | solution.py:46
  119.7 5.5 %collective-permute-done.6 = f32[2,128,128]{2,1,0:T(8,128)S(1)} collective-permute-done((f32[2,128,128]{2,1,0:T(8,128)S(1)}, f32[2,128,128]{2,1,0:T(8,128)S(1)}, u32[]{:S(2)}, u32[]{:S(2)}) %collective-permute-start.6) | collective-permute-done | bytes 131104 | tf_op jit(solution)/shard_map/ppermute | solution.py:45
  126.0 10.7 %all_to_all.20 = f32[2,128,128]{2,0,1:T(2,128)S(1)} all-to-all(f32[2,128,128]{2,0,1:T(2,128)S(1)} %copy.116), channel_id=1, replica_groups=mesh['agent'=2,'row'=8,'col_0'=4,'col_1'=2] {'col_0','col_1'}, dimensions={1} | all-to-all | bytes 262144 | tf_op jit(solution)/shard_map/all_to_all | solution.py:262
  (102 shorter events, 18.6 us)
Async XLA Ops:
  0.6 21.8 %copy-start.1 = (f32[2,2,256,256]{3,2,1,0:T(8,128)S(1)}, f32[2,2,256,256]{3,2,1,0:T(8,128)}, u32[]{:S(2)}) copy-start(f32[2,2,256,256]{3,2,1,0:T(8,128)} %param.12) | copy-start | bytes 3145732
  0.6 59.0 %collective-permute-start = (f32[2,128,128]{2,1,0:T(8,128)}, f32[2,128,128]{2,1,0:T(8,128)S(1)}, u32[]{:S(2)}, u32[]{:S(2)}) collective-permute-start(f32[2,128,128]{2,1,0:T(8,128)} %param.13), channel_id=1, source_target_pairs={{0,8},{8,16},{16,24},{24,32},{32,40},{40,48},{48,56},{56,64},{64,7... | collective-permute-start | bytes 393224 | tf_op jit(solution)/shard_map/ppermute | solution.py:29
  4.6 55.1 %collective-permute-start.1 = (f32[2,128,128]{2,1,0:T(8,128)}, f32[2,128,128]{2,1,0:T(8,128)S(1)}, u32[]{:S(2)}, u32[]{:S(2)}) collective-permute-start(f32[2,128,128]{2,1,0:T(8,128)} %param.13), channel_id=1, source_target_pairs={{8,0},{16,8},{24,16},{32,24},{40,32},{48,40},{56,48},{64,56},{72,6... | collective-permute-start | bytes 393224 | tf_op jit(solution)/shard_map/ppermute | solution.py:32
  10.0 12.8 %collective-permute-start.9 = (bf16[2,6,1024]{2,0,1:T(2,128)(2,1)S(1)}, bf16[2,6,1024]{2,0,1:T(2,128)(2,1)S(1)}, u32[]{:S(2)}, u32[]{:S(2)}) collective-permute-start(bf16[2,6,1024]{2,0,1:T(2,128)(2,1)S(1)} %get-tuple-element.232), channel_id=1, source_target_pairs={{1,0},{2,1},{3,2},{4,3},{5,4},{6,5},{7,6},{8,7},{9,8},{10,9},{11,1... | collective-permute-start | bytes 73736 | tf_op jit(solution)/shard_map/ppermute | solution.py:32
  15.2 9.4 %collective-permute-start.8 = (bf16[2,6,1024]{2,0,1:T(2,128)(2,1)S(1)}, bf16[2,6,1024]{2,0,1:T(2,128)(2,1)S(1)}, u32[]{:S(2)}, u32[]{:S(2)}) collective-permute-start(bf16[2,6,1024]{2,0,1:T(2,128)(2,1)S(1)} %get-tuple-element.231), channel_id=1, source_target_pairs={{0,1},{1,2},{2,3},{3,4},{4,5},{5,6},{6,7},{7,8},{8,9},{9,10},{10,1... | collective-permute-start | bytes 73736 | tf_op jit(solution)/shard_map/ppermute | solution.py:29
  20.4 5.2 %copy-start.8 = (bf16[3,32,6]{1,2,0:T(8,128)(2,1)S(1)}, bf16[3,32,6]{1,2,0:T(8,128)(2,1)}, u32[]{:S(2)}) copy-start(bf16[3,32,6]{1,2,0:T(8,128)(2,1)} %param.15) | copy-start | bytes 3460
  28.5 5.8 %copy-start.9 = (bf16[4,3,32,96]{3,2,1,0:T(8,128)(2,1)S(1)}, bf16[4,3,32,96]{3,2,1,0:T(8,128)(2,1)}, u32[]{:S(2)}) copy-start(bf16[4,3,32,96]{3,2,1,0:T(8,128)(2,1)} %param.16) | copy-start | bytes 221188
  58.5 1.2 copy-start.6
  59.7 10.4 %copy-start.10 = (bf16[3,2,96]{2,1,0:T(2,128)(2,1)S(1)}, bf16[3,2,96]{2,1,0:T(2,128)(2,1)}, u32[]{:S(2)}) copy-start(bf16[3,2,96]{2,1,0:T(2,128)(2,1)} %param.17) | copy-start | bytes 3460
  59.7 11.9 %collective-permute-start.3 = (f32[2,384,128]{2,1,0:T(8,128)S(1)}, f32[2,384,128]{2,1,0:T(8,128)S(1)}, u32[]{:S(2)}, u32[]{:S(2)}) collective-permute-start(f32[2,384,128]{2,1,0:T(8,128)S(1)} %constant_dynamic-update-slice_fusion), channel_id=1, source_target_pairs={{1,0},{2,1},{3,2},{4,3},{5,4},{6,5},{7,6},{9,8},{10,9},{11,10},{12... | collective-permute-start | bytes 1179656 | tf_op jit(solution)/shard_map/ppermute | solution.py:32
  61.0 10.6 %collective-permute-start.2 = (f32[2,384,128]{2,1,0:T(8,128)S(1)}, f32[2,384,128]{2,1,0:T(8,128)S(1)}, u32[]{:S(2)}, u32[]{:S(2)}) collective-permute-start(f32[2,384,128]{2,1,0:T(8,128)S(1)} %constant_dynamic-update-slice_fusion), channel_id=1, source_target_pairs={{0,1},{1,2},{2,3},{3,4},{4,5},{5,6},{6,7},{8,9},{9,10},{10,11},{11... | collective-permute-start | bytes 1179656 | tf_op jit(solution)/shard_map/ppermute | solution.py:29
  89.2 1.3 copy-start
  93.2 6.2 %copy-start.5 = (bf16[32,16,1024]{2,0,1:T(8,128)(2,1)S(1)}, bf16[32,16,1024]{2,0,1:T(8,128)(2,1)}, u32[]{:S(2)}) copy-start(bf16[32,16,1024]{2,0,1:T(8,128)(2,1)} %get-tuple-element.209) | copy-start | bytes 3145732
  94.4 16.7 %collective-permute-start.5 = (f32[2,384,128]{2,1,0:T(8,128)}, f32[2,384,128]{2,1,0:T(8,128)}, u32[]{:S(2)}, u32[]{:S(2)}) collective-permute-start(f32[2,384,128]{2,1,0:T(8,128)} %get-tuple-element.206), channel_id=1, source_target_pairs={{1,0},{2,1},{3,2},{4,3},{5,4},{6,5},{7,6},{9,8},{10,9},{11,10},{12... | collective-permute-start | bytes 1179656 | tf_op jit(solution)/shard_map/ppermute | solution.py:32
  95.7 15.4 %collective-permute-start.4 = (f32[2,384,128]{2,1,0:T(8,128)S(1)}, f32[2,384,128]{2,1,0:T(8,128)}, u32[]{:S(2)}, u32[]{:S(2)}) collective-permute-start(f32[2,384,128]{2,1,0:T(8,128)S(1)} %get-tuple-element.205), channel_id=1, source_target_pairs={{0,1},{1,2},{2,3},{3,4},{4,5},{5,6},{6,7},{8,9},{9,10},{10,11},{11... | collective-permute-start | bytes 1179656 | tf_op jit(solution)/shard_map/ppermute | solution.py:29
  99.5 2.5 %copy-start.2 = (bf16[32,16,1024]{2,0,1:T(8,128)(2,1)S(1)}, bf16[32,16,1024]{2,0,1:T(8,128)(2,1)}, u32[]{:S(2)}) copy-start(bf16[32,16,1024]{2,0,1:T(8,128)(2,1)} %get-tuple-element.207) | copy-start | bytes 3145732
  99.5 2.5 %copy-start.3 = (bf16[32,16,1024]{2,0,1:T(8,128)(2,1)S(1)}, bf16[32,16,1024]{2,0,1:T(8,128)(2,1)}, u32[]{:S(2)}) copy-start(bf16[32,16,1024]{2,0,1:T(8,128)(2,1)} %get-tuple-element.211) | copy-start | bytes 3145732
  99.5 2.5 %copy-start.4 = (bf16[32,16,1024]{2,0,1:T(8,128)(2,1)S(1)}, bf16[32,16,1024]{2,0,1:T(8,128)(2,1)}, u32[]{:S(2)}) copy-start(bf16[32,16,1024]{2,0,1:T(8,128)(2,1)} %get-tuple-element.212) | copy-start | bytes 3145732
  99.5 2.5 %copy-start.7 = (f32[2,16,1024]{2,1,0:T(8,128)S(1)}, f32[2,16,1024]{2,1,0:T(8,128)}, u32[]{:S(2)}) copy-start(f32[2,16,1024]{2,1,0:T(8,128)} %param.14) | copy-start | bytes 393220
  107.7 10.4 %all-to-all-start.1 = ((f32[4,2,2,16,128]{4,1,2,3,0:T(2,128)}), f32[4,2,2,16,128]{4,1,2,3,0:T(2,128)S(1)}, u32[]{:S(2)}, u32[]{:S(2)}) async-start(f32[4,2,2,16,128]{4,1,2,3,0:T(2,128)} %copy.113), calls=%async_computation.1 | async-start | bytes 262144 | tf_op jit(solution)/shard_map/all_to_all | solution.py:72
  112.3 7.5 %collective-permute-start.7 = (f32[2,128,128]{2,1,0:T(8,128)S(1)}, f32[2,128,128]{2,1,0:T(8,128)S(1)}, u32[]{:S(2)}, u32[]{:S(2)}) collective-permute-start(f32[2,128,128]{2,1,0:T(8,128)S(1)} %get-tuple-element.221), channel_id=1, source_target_pairs={{8,0},{16,8},{24,16},{32,24},{40,32},{48,40},{56,48},{64,56},{72,6... | collective-permute-start | bytes 393224 | tf_op jit(solution)/shard_map/ppermute | solution.py:46
  116.2 9.0 %collective-permute-start.6 = (f32[2,128,128]{2,1,0:T(8,128)S(1)}, f32[2,128,128]{2,1,0:T(8,128)S(1)}, u32[]{:S(2)}, u32[]{:S(2)}) collective-permute-start(f32[2,128,128]{2,1,0:T(8,128)S(1)} %get-tuple-element.220), channel_id=1, source_target_pairs={{0,8},{8,16},{16,24},{24,32},{32,40},{40,48},{48,56},{56,64},{64,7... | collective-permute-start | bytes 393224 | tf_op jit(solution)/shard_map/ppermute | solution.py:45
where the time goes:
time: 139 us; the launch traced here: 138 us
  local copies, waits for them, and re-layouts  46.8 us (34%)
  starting transfers between devices  34 us (24%)
  matrix products  23.6 us (17%)
  blocking collectives  14.6 us (11%)
  waiting for transfers between devices  8.79 us (6%)
  other arithmetic  8.58 us (6%)
    slice x6, local copies, waits for them, and re-layouts, convolve(): widened[:, shift_row:shift_row + row_count, shift_col:shift_col + col_count]  27.5 us
    dot_general x18, matrix products, convolve(): jnp.einsum('ok,krw->orw', weight[shift_row], stacked, preferred_element_t...  18 us
    ppermute x4, starting transfers between devices, extended_2(): lax.ppermute(lax.slice_in_dim(block, block.shape[dim] - width, None, axis...  12.7 us
    ppermute x4, starting transfers between devices, extended_2(): lax.ppermute(lax.slice_in_dim(block, 0, width, axis=dim), axis, backward)  12.1 us
    gather x12, local copies, waits for them, and re-layouts  11.3 us
    all_to_all x1, blocking collectives, on_device(): lax.all_to_all(consensus, COL, split_axis=1, concat_axis=2, tiled=True)  10.7 us
    ppermute x1, waiting for transfers between devices, padded(): lax.ppermute(last, axis, up)  5.46 us
    ppermute x1, starting transfers between devices, padded(): lax.ppermute(initial, axis, [(b, a) for a, b in up])  3.9 us
  transfers between devices with their start and end apart: 11, of which 3 were waited for; matrix products, arithmetic and copies ran while one was open for 40% of the time, Pallas kernels for 0%

commit v1 on v0

v1 whole, which is shorter than its diff:
```python
import functools
import math

import jax
import jax.numpy as jnp
import numpy as np
from jax import lax
from jax.experimental import pallas as pl
from jax.experimental.pallas import tpu as pltpu
from jax.sharding import PartitionSpec as P

PROBE = 256
STEP = 64
JITTER = 32
TILE = 128
STRIP = 16
LAYERS = 6
EXT = 384
QUADS = 256
PAIRS = 13
POSITIONS = 4

BF = jnp.bfloat16
F32 = jnp.float32
MESH = pl.DeviceIdType.MESH


def fourier_table():
    numbers = np.arange(PROBE)
    product = (numbers[:, None] * numbers[None, :]) % PROBE
    angles = product * (2.0 * math.pi / PROBE)
    scaling = 1.0 / math.sqrt(PROBE)
    return np.stack([np.cos(angles) * scaling, -np.sin(angles) * scaling]).astype(np.float32)


def dot(left, right):
    return lax.dot_general(left, right, (((1,), (0,)), ((), ())), preferred_element_type=F32)


def dot_nt(left, right):
    return lax.dot_general(left, right, (((1,), (1,)), ((), ())), preferred_element_type=F32)


def slot_of(row, column):
    return column ^ 1 if row else column


def center_lane(row, column):
    return (row // 2) * 256 + (row % 2) * 128 + slot_of(row % 2, column) * 32


def edge_lane(row, column):
    odd = row % 2
    slot = (1 if odd else 0) if column == 4 else (2 if odd else 3)
    return 512 + (row // 2) * 128 + slot * 32


def input_lane(row, column):
    return center_lane(row, column) if 0 <= column < 4 else edge_lane(row, column)


def kernel(
    offsets,
    probe_any,
    amps_any,
    ds_ref,
    ps_any,
    first_ref,
    middle_ref,
    last_ref,
    table_ref,
    data_out,
    prior_out,
    probe,
    amps,
    xf,
    obh,
    obl,
    obr,
    obj,
    acc,
    ff,
    gg,
    ex,
    hs,
    wave,
    cp,
    gsend,
    grecv,
    rsend,
    rrecv,
    drb,
    drs,
    prb,
    prt,
    t1,
    t1r,
    tm,
    t6,
    t6b,
    d2,
    p2,
    xr,
    xv,
    xc,
    a0,
    a1,
    e0,
    e1,
    zz,
    osc,
    local_sem,
    halo_send,
    halo_recv,
    grad_send,
    grad_recv,
    dr_send,
    dr_recv,
    pr_send,
    pr_recv,
):
    agent, row, col = lax.axis_index("agent"), lax.axis_index("row"), lax.axis_index("col")
    tile_row = agent * 8 + row
    strip = tile_row * 8 + col

    def at(tile, column):
        return (lax.div(tile, 8), lax.rem(tile, 8), column)

    up = at(lax.rem(tile_row + 15, 16), col)
    down = at(lax.rem(tile_row + 1, 16), col)
    left = (agent, row, lax.rem(col + 7, 8))
    right = (agent, row, lax.rem(col + 1, 8))
    before, after = lax.rem(strip + 127, 128), lax.rem(strip + 1, 128)
    prev_strip = at(lax.div(before, 8), lax.rem(before, 8))
    next_strip = at(lax.div(after, 8), lax.rem(after, 8))
    peers = [lax.rem(col + k, 8) for k in range(1, 8)]

    def remote(src, dst, send, recv, device):
        return pltpu.make_async_remote_copy(
            src_ref=src, dst_ref=dst, send_sem=send, recv_sem=recv, device_id=device, device_id_type=MESH
        )

    own_strip = pltpu.make_async_copy(ps_any, xf.at[:, 8:24, :], local_sem.at[0])
    own_strip.start()
    load_probe = pltpu.make_async_copy(probe_any, probe, local_sem.at[1])
    load_probe.start()
    load_amps = pltpu.make_async_copy(amps_any, amps, local_sem.at[2])
    load_amps.start()

    barrier = pltpu.get_barrier_semaphore()
    greeted = [up, down, prev_strip, next_strip] + [(agent, row, c) for c in peers]
    for device in greeted:
        pl.semaphore_signal(barrier, inc=1, device_id=device, device_id_type=MESH)
    obh[:, 128:256, :] = ds_ref[...].astype(BF)
    pl.semaphore_wait(barrier, len(greeted))

    to_prev = remote(ps_any.at[:, 0:8, :], xf.at[:, 24:32, :], halo_send.at[0], halo_recv.at[0], prev_strip)
    to_next = remote(ps_any.at[:, 8:16, :], xf.at[:, 0:8, :], halo_send.at[1], halo_recv.at[1], next_strip)
    to_down = remote(obh.at[:, 128:256, :], obh.at[:, 0:128, :], halo_send.at[2], halo_recv.at[2], down)
    to_up = remote(obh.at[:, 128:256, :], obh.at[:, 256:384, :], halo_send.at[3], halo_recv.at[3], up)
    for copy in (to_prev, to_next, to_down, to_up):
        copy.start()

    tm[...] = jnp.zeros_like(tm)
    t6[...] = jnp.zeros_like(t6)
    for r in range(2):
        for c in range(4):
            at_row = r * 128 + slot_of(r, c) * 32
            for a in range(3):
                for b in range(3):
                    lane = input_lane(r + a, c + b - 1)
                    for layer in range(4):
                        tm[layer, at_row : at_row + 32, lane : lane + 32] = middle_ref[
                            layer, a, :, 32 * b : 32 * b + 32
                        ]
                    t6[r * 8 + c * 2 : r * 8 + c * 2 + 2, lane : lane + 32] = last_ref[
                        a, :, 32 * b : 32 * b + 32
                    ].astype(F32)
    t6b[...] = t6[...].astype(BF)

    lane_ids = lax.broadcasted_iota(jnp.int32, (32, 128), 1)
    firsts = [first_ref[a].astype(F32) for a in range(3)]
    for r in range(2):
        for c in range(4):
            at_row = r * 128 + slot_of(r, c) * 32
            parts = [jnp.zeros((32, 128), F32) for _ in range(3)]
            for a in range(3):
                for b in range(3):
                    column = c + b - 1
                    if 0 <= column < 4:
                        block, base = column // 2, (column % 2) * 64
                    else:
                        block, base = 2, 0 if column == 4 else 64
                    for k in range(2):
                        value = firsts[a][:, 2 * b + k : 2 * b + k + 1]
                        parts[block] = jnp.where(lane_ids == base + k * 32 + r + a, value, parts[block])
            for block in range(3):
                t1[at_row : at_row + 32, 128 * block : 128 * block + 128] = parts[block]

    def shift_first(pair, _):
        for block in range(3):
            t1r[pair, :, 128 * block : 128 * block + 128] = pltpu.roll(
                t1[:, 128 * block : 128 * block + 128], 2 + 2 * pair, 1
            ).astype(BF)
        return 0

    lax.fori_loop(0, PAIRS, shift_first, 0)

    vq = lax.broadcasted_iota(jnp.int32, (128, 512), 0)
    jc = lax.broadcasted_iota(jnp.int32, (128, 512), 1)
    hit = lax.rem(jc, 256) == 4 * lax.rem(vq, 64) + 2 * lax.div(vq, 64) + lax.div(jc, 256)
    d2[...] = jnp.where(hit, 1.0, 0.0).astype(BF)
    jq = lax.broadcasted_iota(jnp.int32, (512, 512), 0)
    cc = lax.broadcasted_iota(jnp.int32, (512, 512), 1)
    p2[...] = jnp.where(cc == 4 * lax.rem(jq, 128) + lax.div(jq, 128), 1.0, 0.0).astype(BF)

    real, imag = table_ref[0], table_ref[1]
    minus = (-imag.astype(F32)).astype(BF)
    ff[0:256, 0:256] = real
    ff[0:256, 256:512] = imag
    ff[256:512, 0:256] = minus
    ff[256:512, 256:512] = real
    gg[0:256, 0:256] = real
    gg[0:256, 256:512] = minus
    gg[256:512, 0:256] = imag
    gg[256:512, 256:512] = real

    own_strip.wait()
    to_prev.wait()
    to_next.wait()
    xr[...] = jnp.zeros_like(xr)
    zero_rows = jnp.zeros((8, 128), F32)
    for slot in range(2):
        xv[slot, 0:8, :] = zero_rows
        xv[slot, 264:272, :] = zero_rows
        zz[slot, 0:8, :] = zero_rows
        zz[slot, 264:272, :] = zero_rows
    keep_top = strip > 0
    keep_bottom = strip < 127
    for t in range(4):
        cols = slice(256 * t, 256 * t + 256)
        for k in range(2):
            piece = jnp.concatenate(
                [
                    jnp.where(keep_top, xf[k, 0:8, cols], 0.0),
                    xf[k, 8:24, cols],
                    jnp.where(keep_bottom, xf[k, 24:32, cols], 0.0),
                ],
                axis=0,
            ).astype(BF)
            xr[t, 32 * k : 32 * k + 32, 0:256] = piece
            xr[t, 64 + 32 * k : 96 + 32 * k, 256:512] = piece
        spread = dot_nt(d2[...], xr[t])
        xv[0, 8 + 64 * t : 72 + 64 * t, :] = spread[0:64]
        xv[1, 8 + 64 * t : 72 + 64 * t, :] = spread[64:128]
    wide_ids = lax.broadcasted_iota(jnp.int32, (QUADS, 128), 1)
    low_half = wide_ids < 64
    outer = (wide_ids < 32) | (wide_ids >= 96)
    xc[:, 0:128] = xv[0, 8:264, :].astype(BF)
    xc[:, 128:256] = xv[1, 8:264, :].astype(BF)
    xc[:, 256:384] = jnp.where(low_half, xv[0, 9:265, :], xv[1, 7:263, :]).astype(BF)

    to_down.wait()
    to_up.wait()
    to_right = remote(obh, obl, halo_send.at[4], halo_recv.at[4], right)
    to_left = remote(obh, obr, halo_send.at[5], halo_recv.at[5], left)
    to_right.start()
    to_left.start()

    def finish(y, first, pair, slot, a_out, e_out):
        top = first + 2 * pair
        in_top = (top >= 0) & (top < 2048)
        in_low = (top >= -1) & (top < 2047)
        y0 = jnp.where(in_top, jnp.maximum(y[:, 0:128], 0.0), 0.0)
        y1 = jnp.where(in_low, jnp.maximum(y[:, 128:256], 0.0), 0.0)
        a_out[pair, :, 0:128] = y0.astype(BF)
        a_out[pair, :, 128:256] = y1.astype(BF)
        zz[slot, 8:264, :] = jnp.where(outer, y0, y1)
        e_out[pair] = jnp.where(low_half, zz[slot, 9:265, :], zz[slot, 7:263, :]).astype(BF)

    base = strip * STRIP - LAYERS

    def first_layer(pair, _):
        finish(dot_nt(xc[...], t1r[pair]), base + 1, pair, 0, a0, e0)
        return 0

    lax.fori_loop(0, PAIRS, first_layer, 0)

    def window(a_in, e_in, pair):
        return jnp.concatenate([a_in[pair], a_in[pair + 1], e_in[pair], e_in[pair + 1]], axis=1)

    def middle_layer(depth, a_in, e_in, a_out, e_out):
        def body(pair, _):
            finish(dot_nt(window(a_in, e_in, pair), tm[depth - 2]), base + depth, pair, 0, a_out, e_out)
            return 0

        lax.fori_loop(0, PAIRS + 1 - depth, body, 0)

    middle_layer(2, a0, e0, a1, e1)

    to_right.wait()
    to_left.wait()
    load_probe.wait()
    load_amps.wait()
    for part in range(2):
        for block, source in enumerate((obl, obh, obr)):
            column_in = (col > 0, True, col < 7)[block]
            for third in range(3):
                rows = slice(128 * third, 128 * third + 128)
                if block == 1 and third == 1:
                    value = ds_ref[part]
                else:
                    inside = (tile_row > 0, True, tile_row < 15)[third]
                    keep = jnp.logical_and(inside, column_in)
                    value = jnp.where(keep, source[part, rows, :].astype(F32), 0.0)
                obj[part, block, rows, :] = value
    for part in range(2):
        for block in range(2):
            cp[part, block, 0:128, :] = jnp.zeros((128, 128), F32)
            cp[part, block, 384:512, :] = jnp.zeros((128, 128), F32)
        acc[part] = jnp.zeros((EXT, EXT), F32)

    def position(number, _):
        grid_row, grid_col = lax.div(number, 2), lax.rem(number, 2)
        upper = grid_row * STEP + JITTER + offsets[0, grid_row, grid_col]
        lefty = grid_col * STEP + JITTER + offsets[1, grid_row, grid_col]
        back_roll = lax.rem(EXT - lefty, EXT)
        for chunk in range(0, PROBE, 64):
            rows = slice(chunk, chunk + 64)
            o_r, o_i = [
                pltpu.roll(
                    jnp.concatenate(
                        [obj[part, block, pl.ds(upper + chunk, 64), :] for block in range(3)], axis=1
                    ),
                    back_roll,
                    1,
                )[:, 0:256]
                for part in range(2)
            ]
            p_r, p_i = probe[0, rows, :], probe[1, rows, :]
            ex[rows, 0:256] = (p_r * o_r - p_i * o_i).astype(BF)
            ex[rows, 256:512] = (p_r * o_i + p_i * o_r).astype(BF)
        hs[0:256, :] = dot(ex[...], ff[:, 0:256]).astype(BF)
        hs[256:512, :] = dot(ex[...], ff[:, 256:512]).astype(BF)
        wave[...] = dot(gg[...], hs[...])
        for chunk in range(0, PROBE, 64):
            rows = slice(chunk, chunk + 64)
            w_r, w_i = wave[rows, :], wave[256 + chunk : 320 + chunk, :]
            square = w_r * w_r + w_i * w_i
            retained = 1.0 - amps[number, rows, :] * lax.rsqrt(jnp.maximum(square, 0.25))
            ex[rows, 0:256] = (w_r * retained).astype(BF)
            ex[rows, 256:512] = (w_i * retained).astype(BF)
        hs[0:256, :] = dot(ex[...], gg[:, 0:256]).astype(BF)
        hs[256:512, :] = dot(ex[...], gg[:, 256:512]).astype(BF)
        wave[...] = dot(ff[...], hs[...])
        for chunk in range(0, PROBE, 64):
            rows = slice(chunk, chunk + 64)
            f_r, f_i = wave[rows, :], wave[256 + chunk : 320 + chunk, :]
            p_r, p_i = probe[0, rows, :], probe[1, rows, :]
            for part, term in enumerate((p_r * f_r + p_i * f_i, p_r * f_i - p_i * f_r)):
                for block in range(2):
                    cp[part, block, 128 + chunk : 192 + chunk, :] = term[:, 128 * block : 128 * block + 128]
        for part in range(2):
            for chunk in range(0, EXT, 64):
                term = [cp[part, block, pl.ds(128 - upper + chunk, 64), :] for block in range(2)]
                term = jnp.concatenate(term + [jnp.zeros((64, 128), F32)], axis=1)
                acc[part, chunk : chunk + 64, :] += pltpu.roll(term, lefty, 1)
        return 0

    lax.fori_loop(0, POSITIONS, position, 0)

    for part in range(2):
        gsend[0, part] = acc[part, :, 0:128].astype(BF)
        gsend[1, part] = acc[part, :, 256:384].astype(BF)
    grad_left = remote(gsend.at[0], grecv.at[1], grad_send.at[0], grad_recv.at[0], left)
    grad_right = remote(gsend.at[1], grecv.at[0], grad_send.at[1], grad_recv.at[1], right)
    grad_left.start()
    grad_right.start()

    middle_layer(3, a1, e1, a0, e0)

    grad_left.wait()
    grad_right.wait()
    keeps = (col > 0, col < 7)
    for part in range(2):
        total = acc[part, :, 128:256]
        for side in range(2):
            total = total + jnp.where(keeps[side], grecv[side, part].astype(F32), 0.0)
        acc[part, :, 128:256] = total
        rsend[0, part] = total[0:128].astype(BF)
        rsend[1, part] = total[256:384].astype(BF)
    grad_up = remote(rsend.at[0], rrecv.at[1], grad_send.at[2], grad_recv.at[2], up)
    grad_down = remote(rsend.at[1], rrecv.at[0], grad_send.at[3], grad_recv.at[3], down)
    grad_up.start()
    grad_down.start()

    middle_layer(4, a0, e0, a1, e1)

    grad_up.wait()
    grad_down.wait()
    keeps_row = (tile_row > 0, tile_row < 15)
    for part in range(2):
        total = acc[part, 128:256, 128:256]
        for side in range(2):
            total = total + jnp.where(keeps_row[side], rrecv[side, part].astype(F32), 0.0)
        reflect = ds_ref[part] - 0.25 * total
        acc[part, 128:256, 128:256] = reflect
        drb[part] = reflect.astype(BF)
    dr_copies = []
    for k, c in enumerate(peers):
        dr_copies.append(
            remote(
                drb.at[:, pl.ds(pl.multiple_of(c * STRIP, STRIP), STRIP), :],
                drs.at[col],
                dr_send.at[k],
                dr_recv.at[k],
                (agent, row, c),
            )
        )
        dr_copies[-1].start()
    drs[col] = drb[:, pl.ds(pl.multiple_of(col * STRIP, STRIP), STRIP), :]

    middle_layer(5, a1, e1, a0, e0)

    def last_layer(pair, _):
        y = dot_nt(t6b[...], window(a0, e0, pair))
        for r in range(2):
            for c in range(4):
                for k in range(2):
                    osc[c, pl.ds(k * STRIP + 2 * pair + r, 1), :] = y[r * 8 + c * 2 + k : r * 8 + c * 2 + k + 1, :]
        return 0

    lax.fori_loop(0, STRIP // 2, last_layer, 0)

    for half in range(2):
        joined = jnp.concatenate([osc[c, :, 128 * half : 128 * half + 128] for c in range(4)], axis=1)
        coarse = joined.astype(BF)
        fine = (joined - coarse.astype(F32)).astype(BF)
        both = dot(jnp.concatenate([coarse, fine], axis=0), p2[...])
        noise = both[0:32] + both[32:64]
        for k in range(2):
            cols = slice(512 * half, 512 * half + 512)
            reflect = xf[k, 8:24, cols] - 2.0 * noise[16 * k : 16 * k + 16]
            prior_out[k, :, cols] = 0.5 * xf[k, 8:24, cols] - 0.1 * reflect
            for c in range(4):
                prb[4 * half + c, k] = reflect[:, 128 * c : 128 * c + 128].astype(BF)
    pr_copies = []
    for k, c in enumerate(peers):
        pr_copies.append(remote(prb.at[c], prt.at[col], pr_send.at[k], pr_recv.at[k], (agent, row, c)))
        pr_copies[-1].start()
    prt[col] = prb[col]

    for copy in dr_copies:
        copy.wait()
    for c in range(8):
        cols = slice(128 * c, 128 * c + 128)
        for k in range(2):
            prior_out[k, :, cols] = prior_out[k, :, cols] + 0.6 * drs[c, k].astype(F32)
    for copy in pr_copies:
        copy.wait()
    for c in range(8):
        rows = slice(STRIP * c, STRIP * c + STRIP)
        for k in range(2):
            data_out[k, rows, :] = (
                0.5 * ds_ref[k, rows, :]
                + 0.1 * acc[k, 128 + STRIP * c : 144 + STRIP * c, 128:256]
                + 0.4 * prt[c, k].astype(F32)
            )


def on_device(
    probe_field, offsets, amplitudes, data_state, prior_state, first_weights, middle_weights, last_weights
):
    vmem = pl.BlockSpec(memory_space=pltpu.VMEM)
    anywhere = pl.BlockSpec(memory_space=pl.ANY)
    table = jnp.asarray(fourier_table()).astype(BF)
    dma = pltpu.SemaphoreType.DMA
    return pl.pallas_call(
        kernel,
        name="step",
        out_shape=(
            jax.ShapeDtypeStruct((2, TILE, TILE), F32),
            jax.ShapeDtypeStruct((2, STRIP, 1024), F32),
        ),
        in_specs=[
            pl.BlockSpec(memory_space=pltpu.SMEM),
            anywhere,
            anywhere,
            vmem,
            anywhere,
            vmem,
            vmem,
            vmem,
            vmem,
        ],
        out_specs=(vmem, vmem),
        scratch_shapes=[
            pltpu.VMEM((2, PROBE, PROBE), F32),
            pltpu.VMEM((POSITIONS, PROBE, PROBE), F32),
            pltpu.VMEM((2, 32, 1024), F32),
            pltpu.VMEM((2, EXT, TILE), BF),
            pltpu.VMEM((2, EXT, TILE), BF),
            pltpu.VMEM((2, EXT, TILE), BF),
            pltpu.VMEM((2, 3, EXT, TILE), F32),
            pltpu.VMEM((2, EXT, EXT), F32),
            pltpu.VMEM((512, 512), BF),
            pltpu.VMEM((512, 512), BF),
            pltpu.VMEM((256, 512), BF),
            pltpu.VMEM((512, 256), BF),
            pltpu.VMEM((512, 256), F32),
            pltpu.VMEM((2, 2, 512, 128), F32),
            pltpu.VMEM((2, 2, EXT, TILE), BF),
            pltpu.VMEM((2, 2, EXT, TILE), BF),
            pltpu.VMEM((2, 2, TILE, TILE), BF),
            pltpu.VMEM((2, 2, TILE, TILE), BF),
            pltpu.VMEM((2, TILE, TILE), BF),
            pltpu.VMEM((8, 2, STRIP, TILE), BF),
            pltpu.VMEM((8, 2, STRIP, TILE), BF),
            pltpu.VMEM((8, 2, STRIP, TILE), BF),
            pltpu.VMEM((256, 384), F32),
            pltpu.VMEM((PAIRS, 256, 384), BF),
            pltpu.VMEM((4, 256, 768), BF),
            pltpu.VMEM((16, 768), F32),
            pltpu.VMEM((16, 768), BF),
            pltpu.VMEM((128, 512), BF),
            pltpu.VMEM((512, 512), BF),
            pltpu.VMEM((4, 128, 512), BF),
            pltpu.VMEM((2, 272, 128), F32),
            pltpu.VMEM((256, 384), BF),
            pltpu.VMEM((PAIRS, 256, 256), BF),
            pltpu.VMEM((PAIRS, 256, 256), BF),
            pltpu.VMEM((PAIRS, 256, 128), BF),
            pltpu.VMEM((PAIRS, 256, 128), BF),
            pltpu.VMEM((2, 272, 128), F32),
            pltpu.VMEM((4, 32, 256), F32),
            dma((3,)),
            dma((6,)),
            dma((6,)),
            dma((4,)),
            dma((4,)),
            dma((7,)),
            dma((7,)),
            dma((7,)),
            dma((7,)),
        ],
        compiler_params=pltpu.CompilerParams(
            collective_id=0, has_side_effects=True, vmem_limit_bytes=48 * 1024 * 1024
        ),
    )(
        offsets,
        probe_field,
        amplitudes.reshape(POSITIONS, PROBE, PROBE),
        data_state,
        prior_state,
        first_weights,
        middle_weights,
        last_weights,
        table,
    )


def solution(mesh):
    tiles = P(None, ("agent", "row"), "col")
    strips = P(None, ("agent", "row", "col"), None)
    in_specs = (P(), tiles, P(("agent", "row"), "col", None, None), tiles, strips, P(), P(), P())
    return jax.shard_map(
        on_device, mesh=mesh, in_specs=in_specs, out_specs=(tiles, strips), check_vma=False
    )
```

time: 139 us -> 57.1 us (0.41)
  the two profiles are of different devices: /device:TPU:6 before, /device:TPU:1 now
where the time goes in v1:
time: 57.1 us; the launch traced here: 56.8 us
  Pallas kernels  48.1 us (84%)
  local copies, waits for them, and re-layouts  8.04 us (14%)
  between operations  0.68 us (1%)
    pallas_call x1, Pallas kernels, on_device(): pl.pallas_call(kernel, name='step', out_shape=(jax.ShapeDtypeStruct((2, T...  48.1 us
    unnamed x19, local copies, waits for them, and re-layouts  8.04 us

profile of v1, /device:TPU:1, one launch (start us, length us, event | category | flops | bytes accessed | tf_op | source)
XLA Modules:
  0.0 56.8 jit_solution(323786674519906077)
XLA Ops:
  0.6 0.0 copy-start.6
  0.6 0.0 copy-start.7
  0.7 0.8 %copy.11.first_ref = bf16[3,32,6]{2,1,0:T(8,128)(2,1)S(1)} copy(bf16[3,32,6]{1,2,0:T(8,128)(2,1)} %param.14) | data formatting | bytes 2304 | tf_op args[5]
  1.5 0.0 copy-done.6
  1.5 0.0 copy-done.7
  1.5 0.0 copy-start
  1.5 1.2 %copy-done = f32[2,2,256,256]{3,2,1,0:T(8,128)S(1)} copy-done((f32[2,2,256,256]{3,2,1,0:T(8,128)S(1)}, f32[2,2,256,256]{3,2,1,0:T(8,128)}, u32[]{:S(2)}) %copy-start) | copy-done | bytes 1048600
  2.7 0.0 copy-start.1
  2.7 1.0 %copy-done.1 = f32[2,256,256]{2,1,0:T(8,128)S(1)} copy-done((f32[2,256,256]{2,1,0:T(8,128)S(1)}, f32[2,256,256]{2,1,0:T(8,128)}, u32[]{:S(2)}) %copy-start.1) | copy-done | bytes 524312
  3.8 0.0 copy-start.2
  3.8 0.9 %copy-done.2 = bf16[2,256,256]{2,1,0:T(8,128)(2,1)S(1)} copy-done((bf16[2,256,256]{2,1,0:T(8,128)(2,1)S(1)}, bf16[2,256,256]{2,1,0:T(8,128)(2,1)}, u32[]{:S(2)}) %copy-start.2) | copy-done | bytes 262168
  4.7 0.0 copy-start.3
  4.7 0.9 %copy-done.3 = f32[2,128,128]{2,1,0:T(8,128)S(1)} copy-done((f32[2,128,128]{2,1,0:T(8,128)S(1)}, f32[2,128,128]{2,1,0:T(8,128)}, u32[]{:S(2)}) %copy-start.3) | copy-done | bytes 131096
  5.6 0.0 copy-start.4
  5.6 0.9 %copy-done.4 = f32[2,16,1024]{2,1,0:T(8,128)S(1)} copy-done((f32[2,16,1024]{2,1,0:T(8,128)S(1)}, f32[2,16,1024]{2,1,0:T(8,128)}, u32[]{:S(2)}) %copy-start.4) | copy-done | bytes 131096
  6.5 0.0 copy-start.5
  6.5 0.9 %copy-done.5 = bf16[4,3,32,96]{3,2,1,0:T(8,128)(2,1)S(1)} copy-done((bf16[4,3,32,96]{3,2,1,0:T(8,128)(2,1)S(1)}, bf16[4,3,32,96]{3,2,1,0:T(8,128)(2,1)}, u32[]{:S(2)}) %copy-start.5) | copy-done | bytes 73752
  7.4 48.1 %step.1 = (f32[2,128,128]{2,1,0:T(8,128)S(1)}, f32[2,16,1024]{2,1,0:T(8,128)S(1)}) custom-call(s32[2,2,2]{2,1,0:T(2,128)S(1)} %copy-done.6, f32[2,256,256]{2,1,0:T(8,128)S(1)} %copy-done.1, f32[4,256,256]{2,1,0:T(8,128)S(1)} %bitcast.1, f32[2,128,128]{2,1,0:T(8,128)S(1)} %copy-done.3, f32[2,16,1024]{2,1,0:T(8,128)S(1)} %copy-done.4, ...), custom_call_target="tpu_custom_call" | custom-call | tf_op jit(solution)/shard_map/step/pallas_call | solution.py:478
  55.5 0.7 %copy.14 = f32[2,128,128]{2,1,0:T(8,128)} copy(f32[2,128,128]{2,1,0:T(8,128)S(1)} %get-tuple-element.4) | data formatting | bytes 262144
  56.1 0.7 %copy.15 = f32[2,16,1024]{2,1,0:T(8,128)} copy(f32[2,16,1024]{2,1,0:T(8,128)S(1)} %get-tuple-element.5) | data formatting | bytes 262144
Async XLA Ops:
  0.6 0.8 %copy-start.6 = (s32[2,2,2]{2,1,0:T(2,128)S(1)}, s32[2,2,2]{2,1,0:T(2,128)}, u32[]{:S(2)}) copy-start(s32[2,2,2]{2,1,0:T(2,128)} %offsets.1) | copy-start | bytes 100
  0.6 0.8 %copy-start.7 = (bf16[3,2,96]{2,1,0:T(2,128)(2,1)S(1)}, bf16[3,2,96]{2,1,0:T(2,128)(2,1)}, u32[]{:S(2)}) copy-start(bf16[3,2,96]{2,1,0:T(2,128)(2,1)} %last_ref.1) | copy-start | bytes 3460
  1.5 1.2 %copy-start = (f32[2,2,256,256]{3,2,1,0:T(8,128)S(1)}, f32[2,2,256,256]{3,2,1,0:T(8,128)}, u32[]{:S(2)}) copy-start(f32[2,2,256,256]{3,2,1,0:T(8,128)} %param.11) | copy-start | bytes 3145732
  2.7 1.0 %copy-start.1 = (f32[2,256,256]{2,1,0:T(8,128)S(1)}, f32[2,256,256]{2,1,0:T(8,128)}, u32[]{:S(2)}) copy-start(f32[2,256,256]{2,1,0:T(8,128)} %probe_any.1) | copy-start | bytes 1572868
  3.8 0.9 %copy-start.2 = (bf16[2,256,256]{2,1,0:T(8,128)(2,1)S(1)}, bf16[2,256,256]{2,1,0:T(8,128)(2,1)}, u32[]{:S(2)}) copy-start(bf16[2,256,256]{2,1,0:T(8,128)(2,1)} %constant.6.table_ref) | copy-start | bytes 786436
  4.7 0.9 %copy-start.3 = (f32[2,128,128]{2,1,0:T(8,128)S(1)}, f32[2,128,128]{2,1,0:T(8,128)}, u32[]{:S(2)}) copy-start(f32[2,128,128]{2,1,0:T(8,128)} %ds_ref.1) | copy-start | bytes 393220
  5.6 0.9 %copy-start.4 = (f32[2,16,1024]{2,1,0:T(8,128)S(1)}, f32[2,16,1024]{2,1,0:T(8,128)}, u32[]{:S(2)}) copy-start(f32[2,16,1024]{2,1,0:T(8,128)} %ps_any.1) | copy-start | bytes 393220
  6.5 0.9 %copy-start.5 = (bf16[4,3,32,96]{3,2,1,0:T(8,128)(2,1)S(1)}, bf16[4,3,32,96]{3,2,1,0:T(8,128)(2,1)}, u32[]{:S(2)}) copy-start(bf16[4,3,32,96]{3,2,1,0:T(8,128)(2,1)} %middle_ref.1) | copy-start | bytes 221188

commit v2 on v1

--- a/solution.py
+++ b/solution.py
@@ -63,11 +63,16 @@
     offsets,
     probe_any,
     amps_any,
-    ds_ref,
+    ds_any,
     ps_any,
     first_ref,
+    middle_any,
+    last_ref,
+    table_any,
+    data_any,
+    prior_any,
+    ds_ref,
     middle_ref,
-    last_ref,
     table_ref,
     data_out,
     prior_out,
@@ -77,6 +82,14 @@
     obh,
     obl,
     obr,
+    gsend,
+    grecv,
+    rsend,
+    rrecv,
+    drb,
+    drs,
+    prb,
+    prt,
     obj,
     acc,
     ff,
@@ -85,16 +98,7 @@
     hs,
     wave,
     cp,
-    gsend,
-    grecv,
-    rsend,
-    rrecv,
-    drb,
-    drs,
-    prb,
-    prt,
     t1,
-    t1r,
     tm,
     t6,
     t6b,
@@ -102,7 +106,6 @@
     p2,
     xr,
     xv,
-    xc,
     a0,
     a1,
     e0,
@@ -140,71 +143,87 @@
             src_ref=src, dst_ref=dst, send_sem=send, recv_sem=recv, device_id=device, device_id_type=MESH
         )
 
-    own_strip = pltpu.make_async_copy(ps_any, xf.at[:, 8:24, :], local_sem.at[0])
-    own_strip.start()
-    load_probe = pltpu.make_async_copy(probe_any, probe, local_sem.at[1])
-    load_probe.start()
-    load_amps = pltpu.make_async_copy(amps_any, amps, local_sem.at[2])
-    load_amps.start()
+    loads = [
+        pltpu.make_async_copy(source, target, local_sem.at[k])
+        for k, (source, target) in enumerate(
+            (
+                (ds_any, ds_ref),
+                (ps_any, xf.at[:, 8:24, :]),
+                (middle_any, middle_ref),
+                (table_any, table_ref),
+                (probe_any, probe),
+                (amps_any, amps),
+            )
+        )
+    ]
+    for load in loads:
+        load.start()
 
     barrier = pltpu.get_barrier_semaphore()
     greeted = [up, down, prev_strip, next_strip] + [(agent, row, c) for c in peers]
     for device in greeted:
         pl.semaphore_signal(barrier, inc=1, device_id=device, device_id_type=MESH)
+    loads[0].wait()
+    loads[1].wait()
     obh[:, 128:256, :] = ds_ref[...].astype(BF)
     pl.semaphore_wait(barrier, len(greeted))
 
-    to_prev = remote(ps_any.at[:, 0:8, :], xf.at[:, 24:32, :], halo_send.at[0], halo_recv.at[0], prev_strip)
-    to_next = remote(ps_any.at[:, 8:16, :], xf.at[:, 0:8, :], halo_send.at[1], halo_recv.at[1], next_strip)
+    to_prev = remote(xf.at[:, 8:16, :], xf.at[:, 24:32, :], halo_send.at[0], halo_recv.at[0], prev_strip)
+    to_next = remote(xf.at[:, 16:24, :], xf.at[:, 0:8, :], halo_send.at[1], halo_recv.at[1], next_strip)
     to_down = remote(obh.at[:, 128:256, :], obh.at[:, 0:128, :], halo_send.at[2], halo_recv.at[2], down)
     to_up = remote(obh.at[:, 128:256, :], obh.at[:, 256:384, :], halo_send.at[3], halo_recv.at[3], up)
     for copy in (to_prev, to_next, to_down, to_up):
         copy.start()
 
-    tm[...] = jnp.zeros_like(tm)
+    for load in loads[2:4]:
+        load.wait()
     t6[...] = jnp.zeros_like(t6)
     for r in range(2):
         for c in range(4):
-            at_row = r * 128 + slot_of(r, c) * 32
             for a in range(3):
                 for b in range(3):
                     lane = input_lane(r + a, c + b - 1)
-                    for layer in range(4):
-                        tm[layer, at_row : at_row + 32, lane : lane + 32] = middle_ref[
-                            layer, a, :, 32 * b : 32 * b + 32
-                        ]
                     t6[r * 8 + c * 2 : r * 8 + c * 2 + 2, lane : lane + 32] = last_ref[
                         a, :, 32 * b : 32 * b + 32
                     ].astype(F32)
     t6b[...] = t6[...].astype(BF)
 
-    lane_ids = lax.broadcasted_iota(jnp.int32, (32, 128), 1)
-    firsts = [first_ref[a].astype(F32) for a in range(3)]
-    for r in range(2):
-        for c in range(4):
-            at_row = r * 128 + slot_of(r, c) * 32
-            parts = [jnp.zeros((32, 128), F32) for _ in range(3)]
-            for a in range(3):
-                for b in range(3):
-                    column = c + b - 1
-                    if 0 <= column < 4:
-                        block, base = column // 2, (column % 2) * 64
-                    else:
-                        block, base = 2, 0 if column == 4 else 64
-                    for k in range(2):
-                        value = firsts[a][:, 2 * b + k : 2 * b + k + 1]
-                        parts[block] = jnp.where(lane_ids == base + k * 32 + r + a, value, parts[block])
-            for block in range(3):
-                t1[at_row : at_row + 32, 128 * block : 128 * block + 128] = parts[block]
-
-    def shift_first(pair, _):
-        for block in range(3):
-            t1r[pair, :, 128 * block : 128 * block + 128] = pltpu.roll(
-                t1[:, 128 * block : 128 * block + 128], 2 + 2 * pair, 1
-            ).astype(BF)
-        return 0
-
-    lax.fori_loop(0, PAIRS, shift_first, 0)
+    def banded(value_of, r, line, place, height):
+        slots = lax.broadcasted_iota(jnp.int32, (height, 128), 1) // 32
+        total = jnp.zeros((height, 128), F32)
+        if 0 <= line - r <= 2:
+            for b in range(3):
+                c = place - b + 1
+                if 0 <= c < 4:
+                    total = jnp.where(slots == slot_of(r, c), value_of(line - r, b), total)
+        return total
+
+    for layer in range(4):
+        turned = []
+        for a in range(3):
+            block = jnp.transpose(middle_ref[layer, a].astype(F32))
+            turned.append(jnp.concatenate([block] * 4, axis=1))
+        for line in range(4):
+            for place in range(-1, 5):
+                lane = input_lane(line, place)
+                for r in range(2):
+                    tm[layer, lane : lane + 32, 128 * r : 128 * r + 128] = banded(
+                        lambda a, b: turned[a][32 * b : 32 * b + 32], r, line, place, 32
+                    ).astype(BF)
+
+    t1[...] = jnp.zeros_like(t1)
+    firsts = [jnp.concatenate([first_ref[a].astype(F32)] * 4, axis=1) for a in range(3)]
+    for line in range(4):
+        for place in range(-1, 5):
+            if 0 <= place < 4:
+                lane = (place % 2) * 64 + 4 * (place // 2) + line
+            else:
+                lane = (0 if place == 4 else 64) + 8 + line
+            for k in range(2):
+                for r in range(2):
+                    t1[lane + 32 * k : lane + 32 * k + 1, 128 * r : 128 * r + 128] = banded(
+                        lambda a, b: firsts[a][2 * b + k : 2 * b + k + 1], r, line, place, 1
+                    )
 
     vq = lax.broadcasted_iota(jnp.int32, (128, 512), 0)
     jc = lax.broadcasted_iota(jnp.int32, (128, 512), 1)
@@ -225,7 +244,6 @@
     gg[256:512, 0:256] = imag
     gg[256:512, 256:512] = real
 
-    own_strip.wait()
     to_prev.wait()
     to_next.wait()
     xr[...] = jnp.zeros_like(xr)
@@ -233,6 +251,7 @@
     for slot in range(2):
         xv[slot, 0:8, :] = zero_rows
         xv[slot, 264:272, :] = zero_rows
+    for slot in range(4):
         zz[slot, 0:8, :] = zero_rows
         zz[slot, 264:272, :] = zero_rows
     keep_top = strip > 0
@@ -256,9 +275,6 @@
     wide_ids = lax.broadcasted_iota(jnp.int32, (QUADS, 128), 1)
     low_half = wide_ids < 64
     outer = (wide_ids < 32) | (wide_ids >= 96)
-    xc[:, 0:128] = xv[0, 8:264, :].astype(BF)
-    xc[:, 128:256] = xv[1, 8:264, :].astype(BF)
-    xc[:, 256:384] = jnp.where(low_half, xv[0, 9:265, :], xv[1, 7:263, :]).astype(BF)
 
     to_down.wait()
     to_up.wait()
@@ -279,29 +295,50 @@
         e_out[pair] = jnp.where(low_half, zz[slot, 9:265, :], zz[slot, 7:263, :]).astype(BF)
 
     base = strip * STRIP - LAYERS
-
-    def first_layer(pair, _):
-        finish(dot_nt(xc[...], t1r[pair]), base + 1, pair, 0, a0, e0)
-        return 0
-
-    lax.fori_loop(0, PAIRS, first_layer, 0)
-
-    def window(a_in, e_in, pair):
-        return jnp.concatenate([a_in[pair], a_in[pair + 1], e_in[pair], e_in[pair + 1]], axis=1)
+    within = wide_ids & 31
+    edges = jnp.where(low_half, xv[0, 9:265, :], xv[1, 7:263, :])
+
+    def groups(count):
+        parts = -(-count // 4)
+        bounds = [count * k // parts for k in range(parts + 1)]
+        return list(zip(bounds[:-1], bounds[1:]))
+
+    for low, high in groups(PAIRS):
+        taken = []
+        for pair in range(low, high):
+            shift = 128 - 2 - 2 * pair
+            near = pltpu.roll(xv[0, 8:264, :], shift, 1)
+            far = pltpu.roll(xv[1, 8:264, :], (shift + 4) % 128, 1)
+            rest = pltpu.roll(edges, (shift + 8) % 128, 1)
+            taken.append(jnp.where(within < 4, near, jnp.where(within < 8, far, rest)).astype(BF))
+        y = dot(jnp.concatenate(taken, axis=0), t1[...].astype(BF))
+        for pair in range(low, high):
+            k = pair - low
+            finish(y[256 * k : 256 * k + 256], base + 1, pair, k, a0, e0)
+
+    def window(a_in, e_in, low, high):
+        rows = (high - low) * QUADS
+        parts = [
+            a_in[low:high].reshape(rows, 256),
+            a_in[low + 1 : high + 1].reshape(rows, 256),
+            e_in[low:high].reshape(rows, 128),
+            e_in[low + 1 : high + 1].reshape(rows, 128),
+        ]
+        return jnp.concatenate(parts, axis=1)
 
     def middle_layer(depth, a_in, e_in, a_out, e_out):
-        def body(pair, _):
-            finish(dot_nt(window(a_in, e_in, pair), tm[depth - 2]), base + depth, pair, 0, a_out, e_out)
-            return 0
-
-        lax.fori_loop(0, PAIRS + 1 - depth, body, 0)
+        for low, high in groups(PAIRS + 1 - depth):
+            y = dot(window(a_in, e_in, low, high), tm[depth - 2])
+            for pair in range(low, high):
+                k = pair - low
+                finish(y[256 * k : 256 * k + 256], base + depth, pair, k, a_out, e_out)
 
     middle_layer(2, a0, e0, a1, e1)
 
     to_right.wait()
     to_left.wait()
-    load_probe.wait()
-    load_amps.wait()
+    loads[4].wait()
+    loads[5].wait()
     for part in range(2):
         for block, source in enumerate((obl, obh, obr)):
             column_in = (col > 0, True, col < 7)[block]
@@ -315,15 +352,32 @@
                     value = jnp.where(keep, source[part, rows, :].astype(F32), 0.0)
                 obj[part, block, rows, :] = value
     for part in range(2):
-        for block in range(2):
-            cp[part, block, 0:128, :] = jnp.zeros((128, 128), F32)
-            cp[part, block, 384:512, :] = jnp.zeros((128, 128), F32)
-        acc[part] = jnp.zeros((EXT, EXT), F32)
-
-    def position(number, _):
-        grid_row, grid_col = lax.div(number, 2), lax.rem(number, 2)
-        upper = grid_row * STEP + JITTER + offsets[0, grid_row, grid_col]
-        lefty = grid_col * STEP + JITTER + offsets[1, grid_row, grid_col]
+        for number in range(POSITIONS):
+            for block in range(2):
+                cp[number, part, block, 0:128, :] = jnp.zeros((128, 128), F32)
+                cp[number, part, block, 384:512, :] = jnp.zeros((128, 128), F32)
+
+    places = []
+    for number in range(POSITIONS):
+        grid_row, grid_col = divmod(number, 2)
+        places.append(
+            (
+                grid_row * STEP + JITTER + offsets[0, grid_row, grid_col],
+                grid_col * STEP + JITTER + offsets[1, grid_row, grid_col],
+            )
+        )
+
+    def transform(first, second):
+        for number in range(0, POSITIONS, 2):
+            rows = slice(256 * number, 256 * number + 512)
+            for part in range(2):
+                half = dot(ex[rows, :], first[:, 256 * part : 256 * part + 256]).astype(BF)
+                for k in range(2):
+                    hs[number + k, 256 * part : 256 * part + 256, :] = half[256 * k : 256 * k + 256]
+        for number in range(POSITIONS):
+            wave[number] = dot(second[...], hs[number])
+
+    for number, (upper, lefty) in enumerate(places):
         back_roll = lax.rem(EXT - lefty, EXT)
         for chunk in range(0, PROBE, 64):
             rows = slice(chunk, chunk + 64)
@@ -338,36 +392,39 @@
                 for part in range(2)
             ]
             p_r, p_i = probe[0, rows, :], probe[1, rows, :]
-            ex[rows, 0:256] = (p_r * o_r - p_i * o_i).astype(BF)
-            ex[rows, 256:512] = (p_r * o_i + p_i * o_r).astype(BF)
-        hs[0:256, :] = dot(ex[...], ff[:, 0:256]).astype(BF)
-        hs[256:512, :] = dot(ex[...], ff[:, 256:512]).astype(BF)
-        wave[...] = dot(gg[...], hs[...])
+            out = slice(256 * number + chunk, 256 * number + chunk + 64)
+            ex[out, 0:256] = (p_r * o_r - p_i * o_i).astype(BF)
+            ex[out, 256:512] = (p_r * o_i + p_i * o_r).astype(BF)
+    transform(ff, gg)
+    for number in range(POSITIONS):
         for chunk in range(0, PROBE, 64):
             rows = slice(chunk, chunk + 64)
-            w_r, w_i = wave[rows, :], wave[256 + chunk : 320 + chunk, :]
+            w_r, w_i = wave[number, rows, :], wave[number, 256 + chunk : 320 + chunk, :]
             square = w_r * w_r + w_i * w_i
             retained = 1.0 - amps[number, rows, :] * lax.rsqrt(jnp.maximum(square, 0.25))
-            ex[rows, 0:256] = (w_r * retained).astype(BF)
-            ex[rows, 256:512] = (w_i * retained).astype(BF)
-        hs[0:256, :] = dot(ex[...], gg[:, 0:256]).astype(BF)
-        hs[256:512, :] = dot(ex[...], gg[:, 256:512]).astype(BF)
-        wave[...] = dot(ff[...], hs[...])
+            out = slice(256 * number + chunk, 256 * number + chunk + 64)
+            ex[out, 0:256] = (w_r * retained).astype(BF)
+            ex[out, 256:512] = (w_i * retained).astype(BF)
+    transform(gg, ff)
+    for number, (upper, lefty) in enumerate(places):
         for chunk in range(0, PROBE, 64):
             rows = slice(chunk, chunk + 64)
-            f_r, f_i = wave[rows, :], wave[256 + chunk : 320 + chunk, :]
+            f_r, f_i = wave[number, rows, :], wave[number, 256 + chunk : 320 + chunk, :]
             p_r, p_i = probe[0, rows, :], probe[1, rows, :]
             for part, term in enumerate((p_r * f_r + p_i * f_i, p_r * f_i - p_i * f_r)):
                 for block in range(2):
-                    cp[part, block, 128 + chunk : 192 + chunk, :] = term[:, 128 * block : 128 * block + 128]
-        for part in range(2):
-            for chunk in range(0, EXT, 64):
-                term = [cp[part, block, pl.ds(128 - upper + chunk, 64), :] for block in range(2)]
+                    cp[number, part, block, 128 + chunk : 192 + chunk, :] = term[
+                        :, 128 * block : 128 * block + 128
+                    ]
+    for part in range(2):
+        for chunk in range(0, EXT, 64):
+            total = None
+            for number, (upper, lefty) in enumerate(places):
+                term = [cp[number, part, block, pl.ds(128 - upper + chunk, 64), :] for block in range(2)]
                 term = jnp.concatenate(term + [jnp.zeros((64, 128), F32)], axis=1)
-                acc[part, chunk : chunk + 64, :] += pltpu.roll(term, lefty, 1)
-        return 0
-
-    lax.fori_loop(0, POSITIONS, position, 0)
+                term = pltpu.roll(term, lefty, 1)
+                total = term if total is None else total + term
+            acc[part, chunk : chunk + 64, :] = total
 
     for part in range(2):
         gsend[0, part] = acc[part, :, 0:128].astype(BF)
@@ -422,15 +479,13 @@
 
     middle_layer(5, a1, e1, a0, e0)
 
-    def last_layer(pair, _):
-        y = dot_nt(t6b[...], window(a0, e0, pair))
+    for pair in range(STRIP // 2):
+        y = dot_nt(t6b[...], window(a0, e0, pair, pair + 1))
         for r in range(2):
             for c in range(4):
                 for k in range(2):
-                    osc[c, pl.ds(k * STRIP + 2 * pair + r, 1), :] = y[r * 8 + c * 2 + k : r * 8 + c * 2 + k + 1, :]
-        return 0
-
-    lax.fori_loop(0, STRIP // 2, last_layer, 0)
+                    at_row = k * STRIP + 2 * pair + r
+                    osc[c, at_row : at_row + 1, :] = y[r * 8 + c * 2 + k : r * 8 + c * 2 + k + 1, :]
 
     for half in range(2):
         joined = jnp.concatenate([osc[c, :, 128 * half : 128 * half + 128] for c in range(4)], axis=1)
@@ -456,6 +511,8 @@
         cols = slice(128 * c, 128 * c + 128)
         for k in range(2):
             prior_out[k, :, cols] = prior_out[k, :, cols] + 0.6 * drs[c, k].astype(F32)
+    store_prior = pltpu.make_async_copy(prior_out, prior_any, local_sem.at[8])
+    store_prior.start()
     for copy in pr_copies:
         copy.wait()
     for c in range(8):
@@ -466,13 +523,17 @@
                 + 0.1 * acc[k, 128 + STRIP * c : 144 + STRIP * c, 128:256]
                 + 0.4 * prt[c, k].astype(F32)
             )
+    store_data = pltpu.make_async_copy(data_out, data_any, local_sem.at[9])
+    store_data.start()
+    store_prior.wait()
+    store_data.wait()
 
 
 def on_device(
     probe_field, offsets, amplitudes, data_state, prior_state, first_weights, middle_weights, last_weights
 ):
+    hbm = pl.BlockSpec(memory_space=pltpu.HBM)
     vmem = pl.BlockSpec(memory_space=pltpu.VMEM)
-    anywhere = pl.BlockSpec(memory_space=pl.ANY)
     table = jnp.asarray(fourier_table()).astype(BF)
     dma = pltpu.SemaphoreType.DMA
     return pl.pallas_call(
@@ -484,31 +545,28 @@
         ),
         in_specs=[
             pl.BlockSpec(memory_space=pltpu.SMEM),
-            anywhere,
-            anywhere,
+            hbm,
+            hbm,
+            hbm,
+            hbm,
             vmem,
-            anywhere,
+            hbm,
             vmem,
-            vmem,
-            vmem,
-            vmem,
+            hbm,
         ],
-        out_specs=(vmem, vmem),
+        out_specs=(hbm, hbm),
         scratch_shapes=[
+            pltpu.VMEM((2, TILE, TILE), F32),
+            pltpu.VMEM((4, 3, 32, 96), BF),
+            pltpu.VMEM((2, 256, 256), BF),
+            pltpu.VMEM((2, TILE, TILE), F32),
+            pltpu.VMEM((2, STRIP, 1024), F32),
             pltpu.VMEM((2, PROBE, PROBE), F32),
             pltpu.VMEM((POSITIONS, PROBE, PROBE), F32),
             pltpu.VMEM((2, 32, 1024), F32),
             pltpu.VMEM((2, EXT, TILE), BF),
             pltpu.VMEM((2, EXT, TILE), BF),
             pltpu.VMEM((2, EXT, TILE), BF),
-            pltpu.VMEM((2, 3, EXT, TILE), F32),
-            pltpu.VMEM((2, EXT, EXT), F32),
-            pltpu.VMEM((512, 512), BF),
-            pltpu.VMEM((512, 512), BF),
-            pltpu.VMEM((256, 512), BF),
-            pltpu.VMEM((512, 256), BF),
-            pltpu.VMEM((512, 256), F32),
-            pltpu.VMEM((2, 2, 512, 128), F32),
             pltpu.VMEM((2, 2, EXT, TILE), BF),
             pltpu.VMEM((2, 2, EXT, TILE), BF),
             pltpu.VMEM((2, 2, TILE, TILE), BF),
@@ -517,23 +575,29 @@
             pltpu.VMEM((8, 2, STRIP, TILE), BF),
             pltpu.VMEM((8, 2, STRIP, TILE), BF),
             pltpu.VMEM((8, 2, STRIP, TILE), BF),
-            pltpu.VMEM((256, 384), F32),
-            pltpu.VMEM((PAIRS, 256, 384), BF),
-            pltpu.VMEM((4, 256, 768), BF),
+            pltpu.VMEM((2, 3, EXT, TILE), F32),
+            pltpu.VMEM((2, EXT, EXT), F32),
+            pltpu.VMEM((512, 512), BF),
+            pltpu.VMEM((512, 512), BF),
+            pltpu.VMEM((1024, 512), BF),
+            pltpu.VMEM((4, 512, 256), BF),
+            pltpu.VMEM((4, 512, 256), F32),
+            pltpu.VMEM((4, 2, 2, 512, 128), F32),
+            pltpu.VMEM((128, 256), F32),
+            pltpu.VMEM((4, 768, 256), BF),
             pltpu.VMEM((16, 768), F32),
             pltpu.VMEM((16, 768), BF),
             pltpu.VMEM((128, 512), BF),
             pltpu.VMEM((512, 512), BF),
             pltpu.VMEM((4, 128, 512), BF),
             pltpu.VMEM((2, 272, 128), F32),
-            pltpu.VMEM((256, 384), BF),
             pltpu.VMEM((PAIRS, 256, 256), BF),
             pltpu.VMEM((PAIRS, 256, 256), BF),
             pltpu.VMEM((PAIRS, 256, 128), BF),
             pltpu.VMEM((PAIRS, 256, 128), BF),
-            pltpu.VMEM((2, 272, 128), F32),
+            pltpu.VMEM((4, 272, 128), F32),
             pltpu.VMEM((4, 32, 256), F32),
-            dma((3,)),
+            dma((10,)),
             dma((6,)),
             dma((6,)),
             dma((4,)),
@@ -544,7 +608,7 @@
             dma((7,)),
         ],
         compiler_params=pltpu.CompilerParams(
-            collective_id=0, has_side_effects=True, vmem_limit_bytes=48 * 1024 * 1024
+            collective_id=0, has_side_effects=True, vmem_limit_bytes=61 * 1024 * 1024
         ),
     )(
         offsets,
@@ -552,7 +616,7 @@
         amplitudes.reshape(POSITIONS, PROBE, PROBE),
         data_state,
         prior_state,
-        first_weights,
+        jnp.transpose(first_weights, (0, 2, 1)),
         middle_weights,
         last_weights,
         table,

time: 57.1 us -> 43.7 us (0.77)
  Pallas kernels: 48.1 us -> 40.6 us
  local copies, waits for them, and re-layouts: 8.04 us -> 2.26 us
    pallas_call x1, Pallas kernels: 48.1 us -> 40.6 us  [on_device(): pl.pallas_call(kernel, name='step', out_shape=(jax.ShapeDtypeStruct((2, T...]
    unnamed x19 -> x4, local copies, waits for them, and re-layouts: 8.04 us -> 2.26 us
where the time goes in v2:
time: 43.7 us; the launch traced here: 43.5 us
  Pallas kernels  40.6 us (93%)
  local copies, waits for them, and re-layouts  2.26 us (5%)
  between operations  0.65 us (1%)
    pallas_call x1, Pallas kernels, on_device(): pl.pallas_call(kernel, name='step', out_shape=(jax.ShapeDtypeStruct((2, T...  40.6 us
    unnamed x4, local copies, waits for them, and re-layouts  2.26 us

profile of v2, /device:TPU:1, one launch (start us, length us, event | category | flops | bytes accessed | tf_op | source)
XLA Modules:
  0.0 43.5 jit_solution(6753337127008418778)
XLA Ops:
  0.6 40.6 %step.1 = (f32[2,128,128]{2,1,0:T(8,128)}, f32[2,16,1024]{2,1,0:T(8,128)}) custom-call(s32[2,2,2]{2,1,0:T(2,128)} %offsets.1, f32[2,256,256]{2,1,0:T(8,128)} %probe_any.1, f32[4,256,256]{2,1,0:T(8,128)} %bitcast.2, f32[2,128,128]{2,1,0:T(8,128)} %ds_any.1, f32[2,16,1024]{2,1,0:T(8,128)} %ps_any.1, bf16[3,6,32]{2,1,0:T(8,128)(2,1)} %bitcast.3, ...), custom_call_target="tpu_custom_call" | custom-call | tf_op jit(solution)/shard_map/step/pallas_call | solution.py:539
  41.2 0.0 copy-start
  41.2 1.6 %copy.13 = f32[2,128,128]{2,1,0:T(8,128)} copy(f32[2,128,128]{2,1,0:T(8,128)} %get-tuple-element.4) | data formatting | bytes 262144
  42.8 0.0 copy-done
  42.8 0.7 %copy.14 = f32[2,16,1024]{2,1,0:T(8,128)} copy(f32[2,16,1024]{2,1,0:T(8,128)S(1)} %copy-done) | data formatting | bytes 262144
Async XLA Ops:
  41.2 1.6 %copy-start = (f32[2,16,1024]{2,1,0:T(8,128)S(1)}, f32[2,16,1024]{2,1,0:T(8,128)}, u32[]{:S(2)}) copy-start(f32[2,16,1024]{2,1,0:T(8,128)} %get-tuple-element.5) | copy-start | bytes 393220

commit v3 on v2

--- a/solution.py
+++ b/solution.py
@@ -79,6 +79,8 @@
     probe,
     amps,
     xf,
+    hsend,
+    hrecv,
     obh,
     obl,
     obr,
@@ -166,14 +168,50 @@
     loads[0].wait()
     loads[1].wait()
     obh[:, 128:256, :] = ds_ref[...].astype(BF)
+    for side in range(2):
+        rows = slice(8 + 8 * side, 16 + 8 * side)
+        hsend[side] = jnp.concatenate([xf[0, rows, :], xf[1, rows, :]], axis=0).astype(BF)
     pl.semaphore_wait(barrier, len(greeted))
 
-    to_prev = remote(xf.at[:, 8:16, :], xf.at[:, 24:32, :], halo_send.at[0], halo_recv.at[0], prev_strip)
-    to_next = remote(xf.at[:, 16:24, :], xf.at[:, 0:8, :], halo_send.at[1], halo_recv.at[1], next_strip)
-    to_down = remote(obh.at[:, 128:256, :], obh.at[:, 0:128, :], halo_send.at[2], halo_recv.at[2], down)
-    to_up = remote(obh.at[:, 128:256, :], obh.at[:, 256:384, :], halo_send.at[3], halo_recv.at[3], up)
-    for copy in (to_prev, to_next, to_down, to_up):
-        copy.start()
+    def started(copies):
+        for copy in copies:
+            copy.start()
+        return copies
+
+    def finished(copies):
+        for copy in copies:
+            copy.wait()
+
+    def halo(src, dst, number, device):
+        return remote(src, dst, halo_send.at[number], halo_recv.at[number], device)
+
+    def grad(src, dst, number, device):
+        return remote(src, dst, grad_send.at[number], grad_recv.at[number], device)
+
+    thirds = [slice(128 * k, 128 * k + 128) for k in range(3)]
+    strip_halo = started(
+        [
+            halo(hsend.at[0], hrecv.at[1], 0, prev_strip),
+            halo(hsend.at[1], hrecv.at[0], 1, next_strip),
+        ]
+    )
+    row_halo = []
+    for part in range(2):
+        own = obh.at[part, thirds[1], :]
+        row_halo.append(
+            started(
+                [
+                    halo(own, obh.at[part, thirds[0], :], 2 + 2 * part, down),
+                    halo(own, obh.at[part, thirds[2], :], 3 + 2 * part, up),
+                ]
+            )
+        )
+    col_halo = started(
+        [
+            halo(obh.at[:, thirds[1], :], obl.at[:, thirds[1], :], 6, right),
+            halo(obh.at[:, thirds[1], :], obr.at[:, thirds[1], :], 7, left),
+        ]
+    )
 
     for load in loads[2:4]:
         load.wait()
@@ -244,8 +282,7 @@
     gg[256:512, 0:256] = imag
     gg[256:512, 256:512] = real
 
-    to_prev.wait()
-    to_next.wait()
+    finished(strip_halo)
     xr[...] = jnp.zeros_like(xr)
     zero_rows = jnp.zeros((8, 128), F32)
     for slot in range(2):
@@ -261,9 +298,9 @@
         for k in range(2):
             piece = jnp.concatenate(
                 [
-                    jnp.where(keep_top, xf[k, 0:8, cols], 0.0),
+                    jnp.where(keep_top, hrecv[0, 8 * k : 8 * k + 8, cols].astype(F32), 0.0),
                     xf[k, 8:24, cols],
-                    jnp.where(keep_bottom, xf[k, 24:32, cols], 0.0),
+                    jnp.where(keep_bottom, hrecv[1, 8 * k : 8 * k + 8, cols].astype(F32), 0.0),
                 ],
                 axis=0,
             ).astype(BF)
@@ -276,12 +313,17 @@
     low_half = wide_ids < 64
     outer = (wide_ids < 32) | (wide_ids >= 96)
 
-    to_down.wait()
-    to_up.wait()
-    to_right = remote(obh, obl, halo_send.at[4], halo_recv.at[4], right)
-    to_left = remote(obh, obr, halo_send.at[5], halo_recv.at[5], left)
-    to_right.start()
-    to_left.start()
+    for part in range(2):
+        finished(row_halo[part])
+        for k in (0, 2):
+            rows = obh.at[part, thirds[k], :]
+            number = 8 + 4 * part + 2 * (k // 2)
+            col_halo += started(
+                [
+                    halo(rows, obl.at[part, thirds[k], :], number, right),
+                    halo(rows, obr.at[part, thirds[k], :], number + 1, left),
+                ]
+            )
 
     def finish(y, first, pair, slot, a_out, e_out):
         top = first + 2 * pair
@@ -335,8 +377,7 @@
 
     middle_layer(2, a0, e0, a1, e1)
 
-    to_right.wait()
-    to_left.wait()
+    finished(col_halo)
     loads[4].wait()
     loads[5].wait()
     for part in range(2):
@@ -416,6 +457,7 @@
                     cp[number, part, block, 128 + chunk : 192 + chunk, :] = term[
                         :, 128 * block : 128 * block + 128
                     ]
+    end_copies = []
     for part in range(2):
         for chunk in range(0, EXT, 64):
             total = None
@@ -425,39 +467,84 @@
                 term = pltpu.roll(term, lefty, 1)
                 total = term if total is None else total + term
             acc[part, chunk : chunk + 64, :] = total
-
-    for part in range(2):
         gsend[0, part] = acc[part, :, 0:128].astype(BF)
         gsend[1, part] = acc[part, :, 256:384].astype(BF)
-    grad_left = remote(gsend.at[0], grecv.at[1], grad_send.at[0], grad_recv.at[0], left)
-    grad_right = remote(gsend.at[1], grecv.at[0], grad_send.at[1], grad_recv.at[1], right)
-    grad_left.start()
-    grad_right.start()
+        ends = []
+        for k in (0, 2):
+            for side in range(2):
+                ends.append(
+                    grad(
+                        gsend.at[side, part, thirds[k], :],
+                        grecv.at[1 - side, part, thirds[k], :],
+                        4 * part + k + side,
+                        right if side else left,
+                    )
+                )
+        end_copies.append(started(ends))
+    middle_copies = started(
+        [
+            grad(gsend.at[side, :, thirds[1], :], grecv.at[1 - side, :, thirds[1], :], 8 + side, device)
+            for side, device in enumerate((left, right))
+        ]
+    )
 
     middle_layer(3, a1, e1, a0, e0)
 
-    grad_left.wait()
-    grad_right.wait()
     keeps = (col > 0, col < 7)
+    keeps_row = (tile_row > 0, tile_row < 15)
+
+    def folded(part, k):
+        total = acc[part, thirds[k], 128:256]
+        for side in range(2):
+            total = total + jnp.where(keeps[side], grecv[side, part, thirds[k], :].astype(F32), 0.0)
+        return total
+
+    row_copies = []
     for part in range(2):
-        total = acc[part, :, 128:256]
-        for side in range(2):
-            total = total + jnp.where(keeps[side], grecv[side, part].astype(F32), 0.0)
-        acc[part, :, 128:256] = total
-        rsend[0, part] = total[0:128].astype(BF)
-        rsend[1, part] = total[256:384].astype(BF)
-    grad_up = remote(rsend.at[0], rrecv.at[1], grad_send.at[2], grad_recv.at[2], up)
-    grad_down = remote(rsend.at[1], rrecv.at[0], grad_send.at[3], grad_recv.at[3], down)
-    grad_up.start()
-    grad_down.start()
+        finished(end_copies[part])
+        rsend[0, part] = folded(part, 0).astype(BF)
+        rsend[1, part] = folded(part, 2).astype(BF)
+        row_copies += started(
+            [
+                grad(rsend.at[0, part], rrecv.at[1, part], 10 + 2 * part, up),
+                grad(rsend.at[1, part], rrecv.at[0, part], 11 + 2 * part, down),
+            ]
+        )
 
     middle_layer(4, a0, e0, a1, e1)
 
-    grad_up.wait()
-    grad_down.wait()
-    keeps_row = (tile_row > 0, tile_row < 15)
+    middle_layer(5, a1, e1, a0, e0)
+
+    for pair in range(STRIP // 2):
+        y = dot_nt(t6b[...], window(a0, e0, pair, pair + 1))
+        for r in range(2):
+            for c in range(4):
+                for k in range(2):
+                    at_row = k * STRIP + 2 * pair + r
+                    osc[c, at_row : at_row + 1, :] = y[r * 8 + c * 2 + k : r * 8 + c * 2 + k + 1, :]
+
+    for half in range(2):
+        joined = jnp.concatenate([osc[c, :, 128 * half : 128 * half + 128] for c in range(4)], axis=1)
+        coarse = joined.astype(BF)
+        fine = (joined - coarse.astype(F32)).astype(BF)
+        both = dot(jnp.concatenate([coarse, fine], axis=0), p2[...])
+        noise = both[0:32] + both[32:64]
+        for k in range(2):
+            cols = slice(512 * half, 512 * half + 512)
+            reflect = xf[k, 8:24, cols] - 2.0 * noise[16 * k : 16 * k + 16]
+            prior_out[k, :, cols] = 0.5 * xf[k, 8:24, cols] - 0.1 * reflect
+            for c in range(4):
+                prb[4 * half + c, k] = reflect[:, 128 * c : 128 * c + 128].astype(BF)
+    pr_copies = []
+    for k, c in enumerate(peers):
+        pr_copies.append(remote(prb.at[c], prt.at[col], pr_send.at[k], pr_recv.at[k], (agent, row, c)))
+        pr_copies[-1].start()
+    prt[col] = prb[col]
+
+    finished(middle_copies)
     for part in range(2):
-        total = acc[part, 128:256, 128:256]
+        finished(row_copies[2 * part : 2 * part + 2])
+        total = folded(part, 1)
         for side in range(2):
             total = total + jnp.where(keeps_row[side], rrecv[side, part].astype(F32), 0.0)
         reflect = ds_ref[part] - 0.25 * total
@@ -476,34 +563,6 @@
         )
         dr_copies[-1].start()
     drs[col] = drb[:, pl.ds(pl.multiple_of(col * STRIP, STRIP), STRIP), :]
-
-    middle_layer(5, a1, e1, a0, e0)
-
-    for pair in range(STRIP // 2):
-        y = dot_nt(t6b[...], window(a0, e0, pair, pair + 1))
-        for r in range(2):
-            for c in range(4):
-                for k in range(2):
-                    at_row = k * STRIP + 2 * pair + r
-                    osc[c, at_row : at_row + 1, :] = y[r * 8 + c * 2 + k : r * 8 + c * 2 + k + 1, :]
-
-    for half in range(2):
-        joined = jnp.concatenate([osc[c, :, 128 * half : 128 * half + 128] for c in range(4)], axis=1)
-        coarse = joined.astype(BF)
-        fine = (joined - coarse.astype(F32)).astype(BF)
-        both = dot(jnp.concatenate([coarse, fine], axis=0), p2[...])
-        noise = both[0:32] + both[32:64]
-        for k in range(2):
-            cols = slice(512 * half, 512 * half + 512)
-            reflect = xf[k, 8:24, cols] - 2.0 * noise[16 * k : 16 * k + 16]
-            prior_out[k, :, cols] = 0.5 * xf[k, 8:24, cols] - 0.1 * reflect
-            for c in range(4):
-                prb[4 * half + c, k] = reflect[:, 128 * c : 128 * c + 128].astype(BF)
-    pr_copies = []
-    for k, c in enumerate(peers):
-        pr_copies.append(remote(prb.at[c], prt.at[col], pr_send.at[k], pr_recv.at[k], (agent, row, c)))
-        pr_copies[-1].start()
-    prt[col] = prb[col]
 
     for copy in dr_copies:
         copy.wait()
@@ -564,6 +623,8 @@
             pltpu.VMEM((2, PROBE, PROBE), F32),
             pltpu.VMEM((POSITIONS, PROBE, PROBE), F32),
             pltpu.VMEM((2, 32, 1024), F32),
+            pltpu.VMEM((2, 16, 1024), BF),
+            pltpu.VMEM((2, 16, 1024), BF),
             pltpu.VMEM((2, EXT, TILE), BF),
             pltpu.VMEM((2, EXT, TILE), BF),
             pltpu.VMEM((2, EXT, TILE), BF),
@@ -598,10 +659,10 @@
             pltpu.VMEM((4, 272, 128), F32),
             pltpu.VMEM((4, 32, 256), F32),
             dma((10,)),
-            dma((6,)),
-            dma((6,)),
-            dma((4,)),
-            dma((4,)),
+            dma((16,)),
+            dma((16,)),
+            dma((14,)),
+            dma((14,)),
             dma((7,)),
             dma((7,)),
             dma((7,)),

time: 43.7 us -> 39.2 us (0.90)
  Pallas kernels: 40.6 us -> 36.1 us
    pallas_call x1, Pallas kernels: 40.6 us -> 36.1 us  [on_device(): pl.pallas_call(kernel, name='step', out_shape=(jax.ShapeDtypeStruct((2, T...]
where the time goes in v3:
time: 39.2 us; the launch traced here: 39 us
  Pallas kernels  36.1 us (92%)
  local copies, waits for them, and re-layouts  2.26 us (6%)
  between operations  0.65 us (2%)
    pallas_call x1, Pallas kernels, on_device(): pl.pallas_call(kernel, name='step', out_shape=(jax.ShapeDtypeStruct((2, T...  36.1 us
    unnamed x4, local copies, waits for them, and re-layouts  2.26 us

profile of v3, /device:TPU:1, one launch (start us, length us, event | category | flops | bytes accessed | tf_op | source)
XLA Modules:
  0.0 39.0 jit_solution(16185826759998218790)
XLA Ops:
  0.6 36.1 %step.1 = (f32[2,128,128]{2,1,0:T(8,128)}, f32[2,16,1024]{2,1,0:T(8,128)}) custom-call(s32[2,2,2]{2,1,0:T(2,128)} %offsets.1, f32[2,256,256]{2,1,0:T(8,128)} %probe_any.1, f32[4,256,256]{2,1,0:T(8,128)} %bitcast.2, f32[2,128,128]{2,1,0:T(8,128)} %ds_any.1, f32[2,16,1024]{2,1,0:T(8,128)} %ps_any.1, bf16[3,6,32]{2,1,0:T(8,128)(2,1)} %bitcast.3, ...), custom_call_target="tpu_custom_call" | custom-call | tf_op jit(solution)/shard_map/step/pallas_call | solution.py:598
  36.7 0.0 copy-start
  36.7 1.6 %copy.13 = f32[2,128,128]{2,1,0:T(8,128)} copy(f32[2,128,128]{2,1,0:T(8,128)} %get-tuple-element.4) | data formatting | bytes 262144
  38.3 0.0 copy-done
  38.4 0.7 %copy.14 = f32[2,16,1024]{2,1,0:T(8,128)} copy(f32[2,16,1024]{2,1,0:T(8,128)S(1)} %copy-done) | data formatting | bytes 262144
Async XLA Ops:
  36.7 1.6 %copy-start = (f32[2,16,1024]{2,1,0:T(8,128)S(1)}, f32[2,16,1024]{2,1,0:T(8,128)}, u32[]{:S(2)}) copy-start(f32[2,16,1024]{2,1,0:T(8,128)} %get-tuple-element.5) | copy-start | bytes 393220

commit v4 on v3

--- a/solution.py
+++ b/solution.py
@@ -282,6 +282,18 @@
     gg[256:512, 0:256] = imag
     gg[256:512, 256:512] = real
 
+    for part in range(2):
+        finished(row_halo[part])
+        for k in (0, 2):
+            rows = obh.at[part, thirds[k], :]
+            number = 8 + 4 * part + 2 * (k // 2)
+            col_halo += started(
+                [
+                    halo(rows, obl.at[part, thirds[k], :], number, right),
+                    halo(rows, obr.at[part, thirds[k], :], number + 1, left),
+                ]
+            )
+
     finished(strip_halo)
     xr[...] = jnp.zeros_like(xr)
     zero_rows = jnp.zeros((8, 128), F32)
@@ -312,18 +324,6 @@
     wide_ids = lax.broadcasted_iota(jnp.int32, (QUADS, 128), 1)
     low_half = wide_ids < 64
     outer = (wide_ids < 32) | (wide_ids >= 96)
-
-    for part in range(2):
-        finished(row_halo[part])
-        for k in (0, 2):
-            rows = obh.at[part, thirds[k], :]
-            number = 8 + 4 * part + 2 * (k // 2)
-            col_halo += started(
-                [
-                    halo(rows, obl.at[part, thirds[k], :], number, right),
-                    halo(rows, obr.at[part, thirds[k], :], number + 1, left),
-                ]
-            )
 
     def finish(y, first, pair, slot, a_out, e_out):
         top = first + 2 * pair
@@ -588,6 +588,17 @@
     store_data.wait()
 
 
+def store(data_ref, prior_ref, data_any, prior_any, sems):
+    copies = [
+        pltpu.make_async_copy(source, target, sems.at[k])
+        for k, (source, target) in enumerate(((data_ref, data_any), (prior_ref, prior_any)))
+    ]
+    for copy in copies:
+        copy.start()
+    for copy in copies:
+        copy.wait()
+
+
 def on_device(
     probe_field, offsets, amplitudes, data_state, prior_state, first_weights, middle_weights, last_weights
 ):
@@ -595,13 +606,14 @@
     vmem = pl.BlockSpec(memory_space=pltpu.VMEM)
     table = jnp.asarray(fourier_table()).astype(BF)
     dma = pltpu.SemaphoreType.DMA
-    return pl.pallas_call(
+    shapes = (
+        jax.ShapeDtypeStruct((2, TILE, TILE), F32),
+        jax.ShapeDtypeStruct((2, STRIP, 1024), F32),
+    )
+    results = pl.pallas_call(
         kernel,
         name="step",
-        out_shape=(
-            jax.ShapeDtypeStruct((2, TILE, TILE), F32),
-            jax.ShapeDtypeStruct((2, STRIP, 1024), F32),
-        ),
+        out_shape=shapes,
         in_specs=[
             pl.BlockSpec(memory_space=pltpu.SMEM),
             hbm,
@@ -682,6 +694,14 @@
         last_weights,
         table,
     )
+    return pl.pallas_call(
+        store,
+        name="store",
+        out_shape=shapes,
+        in_specs=[vmem, vmem],
+        out_specs=(hbm, hbm),
+        scratch_shapes=[dma((2,))],
+    )(*results)
 
 
 def solution(mesh):

time: 39.2 us -> 37.5 us (0.957)
  local copies, waits for them, and re-layouts: 2.26 us -> 0 us
  Pallas kernels: 36.1 us -> 36.7 us
    unnamed x4 -> x0, local copies, waits for them, and re-layouts: 2.26 us -> none
    pallas_call x1 -> x2, Pallas kernels: 36.1 us -> 36.7 us  [the longest x1 35 us: on_device(): pl.pallas_call(kernel, name='step', out_shape=shapes, in_specs=[pl.BlockS...]
where the time goes in v4:
time: 37.5 us; the launch traced here: 37.3 us
  Pallas kernels  36.7 us (98%)
  between operations  0.64 us (2%)
    pallas_call x1, Pallas kernels, on_device(): pl.pallas_call(kernel, name='step', out_shape=shapes, in_specs=[pl.BlockS...  35 us
    pallas_call x1, Pallas kernels, on_device(): pl.pallas_call(store, name='store', out_shape=shapes, in_specs=[vmem, vme...  1.68 us

profile of v4, /device:TPU:1, one launch (start us, length us, event | category | flops | bytes accessed | tf_op | source)
XLA Modules:
  0.0 37.3 jit_solution(14705748741274583469)
XLA Ops:
  0.6 35.0 %step.1 = (f32[2,128,128]{2,1,0:T(8,128)}, f32[2,16,1024]{2,1,0:T(8,128)}) custom-call(s32[2,2,2]{2,1,0:T(2,128)} %offsets.1, f32[2,256,256]{2,1,0:T(8,128)} %probe_any.1, f32[4,256,256]{2,1,0:T(8,128)} %bitcast.2, f32[2,128,128]{2,1,0:T(8,128)} %ds_any.1, f32[2,16,1024]{2,1,0:T(8,128)} %ps_any.1, bf16[3,6,32]{2,1,0:T(8,128)(2,1)} %bitcast.3, ...), custom_call_target="tpu_custom_call" | custom-call | tf_op jit(solution)/shard_map/step/pallas_call | solution.py:613
  35.6 1.7 %store.1 = (f32[2,128,128]{2,1,0:T(8,128)}, f32[2,16,1024]{2,1,0:T(8,128)}) custom-call(f32[2,128,128]{2,1,0:T(8,128)} %get-tuple-element.4.data_ref, f32[2,16,1024]{2,1,0:T(8,128)} %get-tuple-element.5.prior_ref), custom_call_target="tpu_custom_call" | custom-call | tf_op jit(solution)/shard_map/store/pallas_call | solution.py:697

commit v5 on v4

--- a/solution.py
+++ b/solution.py
@@ -145,6 +145,10 @@
             src_ref=src, dst_ref=dst, send_sem=send, recv_sem=recv, device_id=device, device_id_type=MESH
         )
 
+    barrier = pltpu.get_barrier_semaphore()
+    greeted = [up, down, prev_strip, next_strip] + [(agent, row, c) for c in peers]
+    for device in greeted:
+        pl.semaphore_signal(barrier, inc=1, device_id=device, device_id_type=MESH)
     loads = [
         pltpu.make_async_copy(source, target, local_sem.at[k])
         for k, (source, target) in enumerate(
@@ -161,16 +165,8 @@
     for load in loads:
         load.start()
 
-    barrier = pltpu.get_barrier_semaphore()
-    greeted = [up, down, prev_strip, next_strip] + [(agent, row, c) for c in peers]
-    for device in greeted:
-        pl.semaphore_signal(barrier, inc=1, device_id=device, device_id_type=MESH)
     loads[0].wait()
-    loads[1].wait()
     obh[:, 128:256, :] = ds_ref[...].astype(BF)
-    for side in range(2):
-        rows = slice(8 + 8 * side, 16 + 8 * side)
-        hsend[side] = jnp.concatenate([xf[0, rows, :], xf[1, rows, :]], axis=0).astype(BF)
     pl.semaphore_wait(barrier, len(greeted))
 
     def started(copies):
@@ -189,12 +185,6 @@
         return remote(src, dst, grad_send.at[number], grad_recv.at[number], device)
 
     thirds = [slice(128 * k, 128 * k + 128) for k in range(3)]
-    strip_halo = started(
-        [
-            halo(hsend.at[0], hrecv.at[1], 0, prev_strip),
-            halo(hsend.at[1], hrecv.at[0], 1, next_strip),
-        ]
-    )
     row_halo = []
     for part in range(2):
         own = obh.at[part, thirds[1], :]
@@ -210,6 +200,17 @@
         [
             halo(obh.at[:, thirds[1], :], obl.at[:, thirds[1], :], 6, right),
             halo(obh.at[:, thirds[1], :], obr.at[:, thirds[1], :], 7, left),
+        ]
+    )
+
+    loads[1].wait()
+    for side in range(2):
+        rows = slice(8 + 8 * side, 16 + 8 * side)
+        hsend[side] = jnp.concatenate([xf[0, rows, :], xf[1, rows, :]], axis=0).astype(BF)
+    strip_halo = started(
+        [
+            halo(hsend.at[0], hrecv.at[1], 0, prev_strip),
+            halo(hsend.at[1], hrecv.at[0], 1, next_strip),
         ]
     )
 
@@ -377,26 +378,30 @@
 
     middle_layer(2, a0, e0, a1, e1)
 
-    finished(col_halo)
-    loads[4].wait()
-    loads[5].wait()
-    for part in range(2):
-        for block, source in enumerate((obl, obh, obr)):
-            column_in = (col > 0, True, col < 7)[block]
-            for third in range(3):
-                rows = slice(128 * third, 128 * third + 128)
-                if block == 1 and third == 1:
-                    value = ds_ref[part]
-                else:
-                    inside = (tile_row > 0, True, tile_row < 15)[third]
-                    keep = jnp.logical_and(inside, column_in)
-                    value = jnp.where(keep, source[part, rows, :].astype(F32), 0.0)
-                obj[part, block, rows, :] = value
-    for part in range(2):
-        for number in range(POSITIONS):
+    def fill(block, third):
+        column_in = (col > 0, True, col < 7)[block]
+        inside = (tile_row > 0, True, tile_row < 15)[third]
+        for part in range(2):
+            if block == 1 and third == 1:
+                value = ds_ref[part]
+            else:
+                source = (obl, obh, obr)[block]
+                keep = jnp.logical_and(inside, column_in)
+                value = jnp.where(keep, source[part, thirds[third], :].astype(F32), 0.0)
+            obj[part, block, thirds[third], :] = value
+
+    for third in range(3):
+        fill(1, third)
+    for number in range(POSITIONS):
+        for part in range(2):
             for block in range(2):
                 cp[number, part, block, 0:128, :] = jnp.zeros((128, 128), F32)
                 cp[number, part, block, 384:512, :] = jnp.zeros((128, 128), F32)
+    finished(loads[4:6])
+    finished(col_halo)
+    for block in (0, 2):
+        for third in range(3):
+            fill(block, third)
 
     places = []
     for number in range(POSITIONS):

time: 37.5 us -> 37.5 us (level)
  no operation moved by 1% of the time
where the time goes in v5:
time: 37.5 us; the launch traced here: 37.3 us
  Pallas kernels  36.6 us (98%)
  between operations  0.64 us (2%)
    pallas_call x1, Pallas kernels, on_device(): pl.pallas_call(kernel, name='step', out_shape=shapes, in_specs=[pl.BlockS...  34.9 us
    pallas_call x1, Pallas kernels, on_device(): pl.pallas_call(store, name='store', out_shape=shapes, in_specs=[vmem, vme...  1.68 us

profile of v5, /device:TPU:1, one launch (start us, length us, event | category | flops | bytes accessed | tf_op | source)
XLA Modules:
  0.0 37.3 jit_solution(7804948349492287907)
XLA Ops:
  0.6 34.9 %step.1 = (f32[2,128,128]{2,1,0:T(8,128)}, f32[2,16,1024]{2,1,0:T(8,128)}) custom-call(s32[2,2,2]{2,1,0:T(2,128)} %offsets.1, f32[2,256,256]{2,1,0:T(8,128)} %probe_any.1, f32[4,256,256]{2,1,0:T(8,128)} %bitcast.2, f32[2,128,128]{2,1,0:T(8,128)} %ds_any.1, f32[2,16,1024]{2,1,0:T(8,128)} %ps_any.1, bf16[3,6,32]{2,1,0:T(8,128)(2,1)} %bitcast.3, ...), custom_call_target="tpu_custom_call" | custom-call | tf_op jit(solution)/shard_map/step/pallas_call | solution.py:618
  35.6 1.7 %store.1 = (f32[2,128,128]{2,1,0:T(8,128)}, f32[2,16,1024]{2,1,0:T(8,128)}) custom-call(f32[2,128,128]{2,1,0:T(8,128)} %get-tuple-element.4.data_ref, f32[2,16,1024]{2,1,0:T(8,128)} %get-tuple-element.5.prior_ref), custom_call_target="tpu_custom_call" | custom-call | tf_op jit(solution)/shard_map/store/pallas_call | solution.py:702
